TPU v7x, 32 devices: a whole 2x2x4 slice. The times are simulated.
32 devices in a mesh: sample: 2 (over y), region: 4 (over x, core), sub: 4 (over z).
Axes of the slice: x: 2, y: 2, z: 4, core: 2. Of those that a mesh axis runs over, the one named last changes fastest.
Arguments:
- densities: bfloat16 [4096, 128], P(('sample', 'region', 'sub')), parts along dimension 0, may hold values from -6 to 6
- cluster_size: int32 [32], P('sample'), parts along dimension 0, may hold values from 1 to 128, 1365 in all
- near_block: bfloat16 [4096, 512], P(('sample', 'region', 'sub')), parts along dimension 0, may hold values from -0.25 to 0.25
- row_factor: bfloat16 [4096, 512], P(('sample', 'region', 'sub')), parts along dimension 0, may hold values from -0.375 to 0.375
- column_factor: bfloat16 [512, 4096], P(None, ('sample', 'region', 'sub')), parts along dimension 1, may hold values from -0.5 to 0.5
Outputs:
- applied: float32 [4096, 128], P(('sample', 'region', 'sub')), parts along dimension 0
There are 2 independent parts, one for each index of `sample`. A program takes and returns all parts, laid end to end along the dimension named above; each array names one. Nothing has to cross between parts.
Inputs may be any that keep to these rules, and one draw needn't show every extreme that they name: `cluster_size`: sizes of the 16 clusters, summing to 1365, with some cluster of exactly 128.
All inputs are finite; a program needn't handle non-finite values.
Results may differ from a plain program's by a relative error of at most 0.0022.
Values may be sent and summed in bfloat16 or wider, within the bound.
No kernel may reach another device: no remote copies, remote signals or barrier semaphores. Data moves between devices by JAX's collectives and lax.ppermute only.
A program may use at most 64 MiB of HBM per device.

v0:
```python
import jax
import jax.numpy as jnp
from jax import lax
from jax.sharding import PartitionSpec as P


def send_coefficients(coefficients):
    return lax.all_to_all(coefficients, ("region", "sub"), split_axis=0, concat_axis=0, tiled=True)


def local(densities, cluster_size, near_block, row_factor, column_factor):
    row_count, load_count = densities.shape
    group_count = lax.axis_size("sub")
    region_count = lax.axis_size("region")
    cluster_count = group_count * region_count
    rank_width = row_factor.shape[1] // cluster_count
    region_id = lax.axis_index("region")
    own_cluster = region_id * group_count + lax.axis_index("sub")
    slot_index = lax.broadcasted_iota(jnp.int32, (row_count, 1), 0)
    own_live = slot_index < cluster_size[own_cluster]
    masked = jnp.where(own_live, densities, jnp.zeros_like(densities))
    near_sum = jnp.dot(
        near_block,
        lax.all_gather(masked, "sub", axis=0, tiled=True),
        preferred_element_type=jnp.float32,
    )
    cluster_ids = jnp.arange(cluster_count, dtype=jnp.int32)
    far_flags = cluster_ids // group_count != region_id
    coefficients = jnp.dot(column_factor, masked, preferred_element_type=jnp.float32).astype(
        jnp.bfloat16
    )
    received = send_coefficients(coefficients)
    rank_flags = jnp.repeat(far_flags, rank_width)[:, None]
    received = jnp.where(rank_flags, received, jnp.zeros_like(received))
    far_sum = jnp.dot(row_factor, received, preferred_element_type=jnp.float32)
    combined = near_sum + far_sum
    return jnp.where(own_live, combined, jnp.zeros_like(combined))


def solution(mesh):
    return jax.shard_map(
        local,
        mesh=mesh,
        in_specs=(
            P(("sample", "region", "sub"), None),
            P("sample"),
            P(("sample", "region", "sub"), None),
            P(("sample", "region", "sub"), None),
            P(None, ("sample", "region", "sub")),
        ),
        out_specs=P(("sample", "region", "sub"), None),
        check_vma=False,
    )
```

profile of v0, /device:TPU:0, one launch (start us, length us, event | category | flops | bytes accessed | tf_op | source)
XLA Modules:
  0.0 28.1 jit_solution(1108674390602110613)
XLA Ops:
  0.0 0.0 copy-start
  0.0 0.0 copy-start.3
  0.0 0.7 %copy-done.3 = s32[16]{0:T(128)S(1)} copy-done((s32[16]{0:T(128)S(1)}, s32[16]{0:T(128)}, u32[]{:S(2)}) %copy-start.3) | copy-done | bytes 88
  0.7 0.6 %dynamic_slice.3 = s32[1]{0:T(128)} dynamic-slice(s32[16]{0:T(128)S(1)} %copy-done.3, s32[]{:T(128)S(6)} %select_n.23), dynamic_slice_sizes={1} | dynamic-slice | bytes 12 | tf_op jit(solution)/shard_map/dynamic_slice | solution.py:20
  1.3 0.6 %iota_compare_fusion = pred[128]{0:T(512)(128)(4,1)S(1)} fusion(s32[]{:T(128)} %bitcast), kind=kLoop, calls=%fused_computation.12 | loop fusion | flops 128 | bytes 132 | tf_op jit(solution)/shard_map/lt | solution.py:20
  1.9 0.8 %broadcast_select_fusion = bf16[128,128]{1,0:T(8,128)(2,1)S(1)} fusion(bf16[128,128]{1,0:T(8,128)(2,1)} %param.5, pred[128]{0:T(512)(128)(4,1)S(1)} %iota_compare_fusion), kind=kLoop, calls=%fused_computation.6 | loop fusion | flops 16384 | bytes 65664 | tf_op jit(solution)/shard_map/jit(_where)/select_n | solution.py:21
  2.8 0.0 copy-done
  2.8 0.2 fusion
  3.0 0.7 %copy.7 = bf16[512,128]{1,0:T(8,128)(2,1)} copy(bf16[512,128]{0,1:T(8,128)(2,1)S(1)} %fusion) | data formatting | bytes 262144 | tf_op jit(solution)/shard_map/convert_element_type | solution.py:29
  3.8 7.4 %all-to-all-start = ((bf16[16,32,128]{2,1,0:T(8,128)(2,1)}), bf16[16,32,128]{2,1,0:T(8,128)(2,1)S(1)}, u32[]{:S(2)}, u32[]{:S(2)}) async-start(bf16[16,32,128]{2,1,0:T(8,128)(2,1)} %bitcast.2), calls=%async_computation | async-start | bytes 262144 | tf_op jit(solution)/shard_map/all_to_all | solution.py:8
  11.2 0.0 copy-start.1
  11.2 14.7 %all_gather.3 = bf16[512,128]{1,0:T(8,128)(2,1)S(1)} all-gather(bf16[128,128]{1,0:T(8,128)(2,1)S(1)} %broadcast_select_fusion), channel_id=1, replica_groups=mesh['sample'=2,'region'=4,'sub'=4] {'sub'}, dimensions={0}, use_global_device_ids=true | all-gather | bytes 163840 | tf_op jit(solution)/shard_map/all_gather | solution.py:24
  25.8 0.1 broadcast_in_dim.41
  25.9 0.1 broadcast_in_dim.42
  26.0 0.0 copy-done.1
  26.0 0.2 fusion.4
  26.2 0.0 copy-start.2
  26.2 0.0 all-to-all-done
  26.3 0.1 bitcast_select_fusion
  26.4 0.7 %copy-done.2 = bf16[128,512]{1,0:T(8,128)(2,1)S(1)} copy-done((bf16[128,512]{1,0:T(8,128)(2,1)S(1)}, bf16[128,512]{1,0:T(8,128)(2,1)}, u32[]{:S(2)}) %copy-start.2) | copy-done | bytes 131096
  27.1 0.2 fusion.2
  27.4 0.7 %copy.8 = f32[128,128]{1,0:T(8,128)} copy(f32[128,128]{0,1:T(8,128)S(1)} %fusion.2) | data formatting | bytes 131072 | tf_op jit(solution)/shard_map/jit(_where)/select_n | solution.py:37
  (1 shorter events, 0.0 us)
Async XLA Ops:
  0.0 2.8 %copy-start = (bf16[512,128]{1,0:T(8,128)(2,1)S(1)}, bf16[512,128]{1,0:T(8,128)(2,1)}, u32[]{:S(2)}) copy-start(bf16[512,128]{1,0:T(8,128)(2,1)} %param.9) | copy-start | bytes 393220
  0.0 0.7 %copy-start.3 = (s32[16]{0:T(128)S(1)}, s32[16]{0:T(128)}, u32[]{:S(2)}) copy-start(s32[16]{0:T(128)} %param.6) | copy-start | bytes 196
  3.8 22.5 %all-to-all-start = ((bf16[16,32,128]{2,1,0:T(8,128)(2,1)}), bf16[16,32,128]{2,1,0:T(8,128)(2,1)S(1)}, u32[]{:S(2)}, u32[]{:S(2)}) async-start(bf16[16,32,128]{2,1,0:T(8,128)(2,1)} %bitcast.2), calls=%async_computation | async-start | bytes 262144 | tf_op jit(solution)/shard_map/all_to_all | solution.py:8
  11.2 14.9 %copy-start.1 = (bf16[128,512]{1,0:T(8,128)(2,1)S(1)}, bf16[128,512]{1,0:T(8,128)(2,1)}, u32[]{:S(2)}) copy-start(bf16[128,512]{1,0:T(8,128)(2,1)} %param.7) | copy-start | bytes 393220
  26.2 0.9 %copy-start.2 = (bf16[128,512]{1,0:T(8,128)(2,1)S(1)}, bf16[128,512]{1,0:T(8,128)(2,1)}, u32[]{:S(2)}) copy-start(bf16[128,512]{1,0:T(8,128)(2,1)} %param.8) | copy-start | bytes 393220
where the time goes:
time: 28.4 us; the launch traced here: 28.1 us
  blocking collectives  14.7 us (52%)
  starting transfers between devices  7.39 us (26%)
  local copies, waits for them, and re-layouts  3.67 us (13%)
  other arithmetic  1.64 us (6%)
  matrix products  0.65 us (2%)
    all_gather x1, blocking collectives, local(): lax.all_gather(masked, 'sub', axis=0, tiled=True)  14.7 us
    all_to_all x1, starting transfers between devices, send_coefficients(): lax.all_to_all(coefficients, ('region', 'sub'), split_axis=0, concat_axis...  7.39 us
    unnamed x8, local copies, waits for them, and re-layouts  1.45 us
    select_n x1, other arithmetic, local(): masked = jnp.where(own_live, densities, jnp.zeros_like(densities))  0.84 us
    convert_element_type x1, local copies, waits for them, and re-layouts, local(): jnp.dot(column_factor, masked, preferred_element_type=jnp.float32)  0.75 us
    select_n x1, local copies, waits for them, and re-layouts, local(): return jnp.where(own_live, combined, jnp.zeros_like(combined))  0.73 us
    lt x1, other arithmetic, local(): own_live = slot_index < cluster_size[own_cluster]  0.65 us
    dynamic_slice x1, local copies, waits for them, and re-layouts, local(): own_live = slot_index < cluster_size[own_cluster]  0.58 us
  transfers between devices with their start and end apart: 1, of which 0 were waited for; matrix products, arithmetic and copies ran while one was open for 1% of the time, Pallas kernels for 0%

commit v1 on v0

v1 whole, which is shorter than its diff:
```python
import jax
import jax.numpy as jnp
from jax import lax
from jax.experimental import pallas as pl
from jax.experimental.pallas import tpu as pltpu
from jax.sharding import PartitionSpec as P


VMEM = pl.BlockSpec(memory_space=pltpu.VMEM)
HBM = pl.BlockSpec(memory_space=pltpu.HBM)
SMEM = pl.BlockSpec(memory_space=pltpu.SMEM)
PARAMS = pltpu.CompilerParams(vmem_limit_bytes=8 << 20)


def cost(flops):
    return pl.CostEstimate(flops=flops, bytes_accessed=0, transcendentals=0)


def at(start, size):
    return pl.ds(pl.multiple_of(start, size), size)


def local(densities, cluster_size, near_block, row_factor, column_factor):
    slots, loads = densities.shape
    groups = lax.axis_size("sub")
    regions = lax.axis_size("region")
    clusters = groups * regions
    rank = row_factor.shape[1] // clusters
    height = groups * rank
    width = (regions - 1) * rank
    bf16, f32 = jnp.bfloat16, jnp.float32
    hops = range(regions - 1, 0, -1)

    def ahead(sub, step):
        return lax.rem(sub + step, groups)

    def behind(sub, step):
        return lax.rem(sub + groups - step, groups)

    def across(region, hop):
        return lax.bitwise_xor(region, jnp.int32(hop))

    def gather(dens, col, *refs):
        outs, (dens_buf, col_buf, sems) = refs[:groups], refs[groups:]
        sub = lax.axis_index("sub")
        region = lax.axis_index("region")
        first = pltpu.make_async_copy(dens, dens_buf, sems.at[0])
        first.start()
        copies = []
        for step in range(groups):
            goal = ahead(sub, step)
            copies.append(pltpu.make_async_copy(col.at[:, goal], col_buf.at[step], sems.at[1]))
            copies[-1].start()
        first.wait()
        for step in range(groups):
            outs[step][0:slots, :] = dens_buf[...]
        for copy in copies:
            copy.wait()
        for step in range(groups):
            for hop in range(1, regions):
                low = slots + (hop - 1) * rank
                outs[step][low : low + rank, :] = col_buf[step, across(region, hop)]

    parcels = pl.pallas_call(
        gather,
        out_shape=[jax.ShapeDtypeStruct((slots + width, loads), bf16)] * groups,
        in_specs=[HBM] * 2,
        out_specs=[VMEM] * groups,
        scratch_shapes=[
            pltpu.VMEM((slots, loads), bf16),
            pltpu.VMEM((groups, regions, rank, slots), bf16),
            pltpu.SemaphoreType.DMA((2,)),
        ],
        compiler_params=PARAMS,
        name="gather",
    )(
        pltpu.with_memory_space_constraint(densities, pltpu.HBM),
        pltpu.with_memory_space_constraint(column_factor.reshape(regions, groups, rank, slots), pltpu.HBM),
    )

    held = [parcels[0]]
    for step in range(1, groups):
        pairs = [(z, (z + step) % groups) for z in range(groups)]
        held.append(lax.ppermute(parcels[step], "sub", pairs))

    def mask(size_ref, group_ref, own_ref):
        sub = lax.axis_index("sub")
        region = lax.axis_index("region")
        slot = lax.broadcasted_iota(jnp.int32, (slots, loads), 0)
        for g in range(groups):
            keep = slot < size_ref[region * groups + g]
            group_ref[g * slots : (g + 1) * slots, :] = jnp.where(keep, 1.0, 0.0).astype(bf16)
        own_ref[...] = jnp.where(slot < size_ref[region * groups + sub], 1.0, 0.0)

    group_mask, own_mask = pl.pallas_call(
        mask,
        out_shape=[
            jax.ShapeDtypeStruct((groups * slots, loads), bf16),
            jax.ShapeDtypeStruct((slots, loads), f32),
        ],
        in_specs=[SMEM],
        out_specs=[VMEM] * 2,
        compiler_params=PARAMS,
        cost_estimate=cost(1 << 20),
        name="mask",
    )(cluster_size)

    def regroup(mask_ref, *refs):
        ins, outs, rows_ref = refs[:groups], refs[groups:-1], refs[-1]
        sub = lax.axis_index("sub")
        for step in range(groups):
            origin = behind(sub, step)
            here = at(origin * slots, slots)
            rows = ins[step][0:slots, :] * mask_ref[here, :]
            rows_ref[here, :] = rows
            part = jnp.dot(ins[step][slots:, :], rows, preferred_element_type=f32).astype(bf16)
            for hop in range(1, regions):
                outs[hop - 1][at(origin * rank, rank), :] = part[(hop - 1) * rank : hop * rank, :]

    *letters, group_rows = pl.pallas_call(
        regroup,
        out_shape=[jax.ShapeDtypeStruct((height, loads), bf16)] * (regions - 1)
        + [jax.ShapeDtypeStruct((groups * slots, loads), bf16)],
        in_specs=[VMEM] * (groups + 1),
        out_specs=[VMEM] * regions,
        compiler_params=PARAMS,
        cost_estimate=cost(1 << 20),
        name="regroup",
    )(group_mask, *held)

    received = {}
    for hop in hops:
        pairs = [(r, r ^ hop) for r in range(regions)]
        received[hop] = lax.ppermute(letters[hop - 1], "region", pairs)

    def near(block_ref, rows_ref, out):
        out[...] = jnp.dot(block_ref[...], rows_ref[...], preferred_element_type=f32)

    near_sum = pl.pallas_call(
        near,
        out_shape=jax.ShapeDtypeStruct((slots, loads), f32),
        in_specs=[VMEM] * 2,
        out_specs=VMEM,
        compiler_params=PARAMS,
        cost_estimate=cost(1 << 24),
        name="near",
    )(near_block, group_rows)

    def finish(mask_ref, near_ref, factor_ref, *refs):
        ins, out, scratch = refs[: regions - 1], refs[regions - 1], refs[regions]
        region = lax.axis_index("region")
        scratch[at(region * height, height), :] = jnp.zeros((height, loads), bf16)
        for hop in range(1, regions):
            scratch[at(across(region, hop) * height, height), :] = ins[hop - 1][...]
        far = jnp.dot(factor_ref[...], scratch[...], preferred_element_type=f32)
        out[...] = jnp.where(mask_ref[...] > 0.0, near_ref[...] + far, 0.0)

    return pl.pallas_call(
        finish,
        out_shape=jax.ShapeDtypeStruct((slots, loads), f32),
        in_specs=[VMEM] * (regions + 2),
        out_specs=VMEM,
        scratch_shapes=[pltpu.VMEM((clusters * rank, loads), bf16)],
        compiler_params=PARAMS,
        cost_estimate=cost(1 << 24),
        name="finish",
    )(own_mask, near_sum, row_factor, *(received[hop] for hop in range(1, regions)))


def solution(mesh):
    spec = P(("sample", "region", "sub"), None)
    return jax.shard_map(
        local,
        mesh=mesh,
        in_specs=(spec, P("sample"), spec, spec, P(None, ("sample", "region", "sub"))),
        out_specs=spec,
        check_vma=False,
    )
```

time: 28.4 us -> 17.2 us (0.61)
  blocking collectives: 14.7 us -> 0 us
  waiting for transfers between devices: 0.01 us -> 5.35 us
  local copies, waits for them, and re-layouts: 3.67 us -> 0.01 us
  Pallas kernels: 0 us -> 2.61 us
  other arithmetic: 1.64 us -> 0 us
  starting transfers between devices: 7.39 us -> 8.96 us
  matrix products: 0.65 us -> 0 us
    all_gather x1 -> x0, blocking collectives: 14.7 us -> none  [local(): lax.all_gather(masked, 'sub', axis=0, tiled=True)]
    ppermute x0 -> x6, starting transfers between devices: none -> 8.96 us  [the longest x3 7.04 us: local(): held.append(lax.ppermute(parcels[step], 'sub', pairs))]
    all_to_all x1 -> x0, starting transfers between devices: 7.39 us -> none  [send_coefficients(): lax.all_to_all(coefficients, ('region', 'sub'), split_axis=0, concat_axis...]
    ppermute x0 -> x6, waiting for transfers between devices: none -> 5.35 us  [the longest x3 2.91 us: local(): received[hop] = lax.ppermute(letters[hop - 1], 'region', pairs)]
    pallas_call x0 -> x5, Pallas kernels: none -> 2.61 us  [the longest x1 0.84 us: local(): pl.pallas_call(gather, out_shape=[jax.ShapeDtypeStruct((slots + width, lo...]
    unnamed x8 -> x6, local copies, waits for them, and re-layouts: 1.45 us -> 0.01 us
    select_n x2 -> x0, other arithmetic: 0.98 us -> none  [the longest x1 0.84 us: local(): masked = jnp.where(own_live, densities, jnp.zeros_like(densities))]
    convert_element_type x1 -> x0, local copies, waits for them, and re-layouts: 0.75 us -> none  [local(): jnp.dot(column_factor, masked, preferred_element_type=jnp.float32)]
  transfers between devices with their start and end apart: 1 -> 6, of which waited for: 0 -> 4; matrix products, arithmetic and copies ran while one was open for 1% -> 0% of each run, Pallas kernels for 0% -> 4%
where the time goes in v1:
time: 17.2 us; the launch traced here: 17 us
  starting transfers between devices  8.96 us (52%)
  waiting for transfers between devices  5.35 us (31%)
  Pallas kernels  2.61 us (15%)
    ppermute x3, starting transfers between devices, local(): held.append(lax.ppermute(parcels[step], 'sub', pairs))  7.04 us
    ppermute x3, waiting for transfers between devices, local(): received[hop] = lax.ppermute(letters[hop - 1], 'region', pairs)  2.91 us
    ppermute x3, waiting for transfers between devices, local(): held.append(lax.ppermute(parcels[step], 'sub', pairs))  2.45 us
    ppermute x3, starting transfers between devices, local(): received[hop] = lax.ppermute(letters[hop - 1], 'region', pairs)  1.92 us
    pallas_call x1, Pallas kernels, local(): pl.pallas_call(gather, out_shape=[jax.ShapeDtypeStruct((slots + width, lo...  0.84 us
    pallas_call x1, Pallas kernels, local(): pl.pallas_call(finish, out_shape=jax.ShapeDtypeStruct((slots, loads), f32...  0.83 us
    pallas_call x1, Pallas kernels, local(): pl.pallas_call(mask, out_shape=[jax.ShapeDtypeStruct((groups * slots, loa...  0.59 us
  transfers between devices with their start and end apart: 6, of which 4 were waited for; matrix products, arithmetic and copies ran while one was open for 0% of the time, Pallas kernels for 4%

profile of v1, /device:TPU:0, one launch (start us, length us, event | category | flops | bytes accessed | tf_op | source)
XLA Modules:
  0.0 17.0 jit_solution(10403170086266543046)
XLA Ops:
  0.0 0.8 %gather.1 = (bf16[224,128]{1,0:T(8,128)(2,1)S(1)}, bf16[224,128]{1,0:T(8,128)(2,1)S(1)}, bf16[224,128]{1,0:T(8,128)(2,1)S(1)}, bf16[224,128]{1,0:T(8,128)(2,1)S(1)}) custom-call(bf16[128,128]{1,0:T(8,128)(2,1)} %dens.1, bf16[4,4,32,128]{3,2,1,0:T(8,128)(2,1)} %bitcast.1), custom_call_target="tpu_custom_call" | custom-call | tf_op jit(solution)/shard_map/gather/pallas_call | solution.py:64
  0.9 3.1 %collective-permute-start = (bf16[224,128]{1,0:T(8,128)(2,1)S(1)}, bf16[224,128]{1,0:T(8,128)(2,1)S(1)}, u32[]{:S(2)}, u32[]{:S(2)}) collective-permute-start(bf16[224,128]{1,0:T(8,128)(2,1)S(1)} %get-tuple-element.18), channel_id=1, source_target_pairs={{0,1},{1,2},{2,3},{3,0},{4,5},{5,6},{6,7},{7,4},{8,9},{9,10},{10,1... | collective-permute-start | bytes 172040 | tf_op jit(solution)/shard_map/ppermute | solution.py:84
  4.0 0.0 copy-start.2
  4.0 2.6 %collective-permute-start.1 = (bf16[224,128]{1,0:T(8,128)(2,1)S(1)}, bf16[224,128]{1,0:T(8,128)(2,1)S(1)}, u32[]{:S(2)}, u32[]{:S(2)}) collective-permute-start(bf16[224,128]{1,0:T(8,128)(2,1)S(1)} %get-tuple-element.19), channel_id=1, source_target_pairs={{0,2},{1,3},{2,0},{3,1},{4,6},{5,7},{6,4},{7,5},{8,10},{9,11},{10,... | collective-permute-start | bytes 172040 | tf_op jit(solution)/shard_map/ppermute | solution.py:84
  6.5 1.3 %collective-permute-start.2 = (bf16[224,128]{1,0:T(8,128)(2,1)S(1)}, bf16[224,128]{1,0:T(8,128)(2,1)S(1)}, u32[]{:S(2)}, u32[]{:S(2)}) collective-permute-start(bf16[224,128]{1,0:T(8,128)(2,1)S(1)} %get-tuple-element.20), channel_id=1, source_target_pairs={{0,3},{1,0},{2,1},{3,2},{4,7},{5,4},{6,5},{7,6},{8,11},{9,8},{10,9... | collective-permute-start | bytes 172040 | tf_op jit(solution)/shard_map/ppermute | solution.py:84
  7.9 0.0 copy-done.2
  7.9 0.6 %mask.1 = (bf16[512,128]{1,0:T(8,128)(2,1)S(1)}, f32[128,128]{1,0:T(8,128)S(1)}) custom-call(s32[16]{0:T(128)S(1)} %copy-done.2), custom_call_target="tpu_custom_call" | custom-call | flops 1048576 | tf_op jit(solution)/shard_map/mask/pallas_call | solution.py:95
  8.5 0.0 collective-permute-done.refs_1_
  8.5 2.1 %collective-permute-done.1.refs_2_ = bf16[224,128]{1,0:T(8,128)(2,1)S(1)} collective-permute-done((bf16[224,128]{1,0:T(8,128)(2,1)S(1)}, bf16[224,128]{1,0:T(8,128)(2,1)S(1)}, u32[]{:S(2)}, u32[]{:S(2)}) %collective-permute-start.1) | collective-permute-done | bytes 57376 | tf_op jit(solution)/shard_map/ppermute | solution.py:84
  10.6 0.4 %collective-permute-done.2.refs_3_ = bf16[224,128]{1,0:T(8,128)(2,1)S(1)} collective-permute-done((bf16[224,128]{1,0:T(8,128)(2,1)S(1)}, bf16[224,128]{1,0:T(8,128)(2,1)S(1)}, u32[]{:S(2)}, u32[]{:S(2)}) %collective-permute-start.2) | collective-permute-done | bytes 57376 | tf_op jit(solution)/shard_map/ppermute | solution.py:84
  11.0 0.0 copy-start
  11.0 0.2 %regroup.1 = (bf16[128,128]{1,0:T(8,128)(2,1)S(1)}, bf16[128,128]{1,0:T(8,128)(2,1)S(1)}, bf16[128,128]{1,0:T(8,128)(2,1)S(1)}, bf16[512,128]{1,0:T(8,128)(2,1)S(1)}) custom-call(bf16[512,128]{1,0:T(8,128)(2,1)S(1)} %get-tuple-element.16.mask_ref, bf16[224,128]{1,0:T(8,128)(2,1)S(1)} %get-tuple-element.17.refs_0_, ...), custom_call_target="tpu_custom_call" | custom-call | flops 1048576 | tf_op jit(solution)/shard_map/regroup/pallas_call | solution.py:120
  11.1 0.1 collective-permute-start.3
  11.2 1.6 %collective-permute-start.4 = (bf16[128,128]{1,0:T(8,128)(2,1)S(1)}, bf16[128,128]{1,0:T(8,128)(2,1)S(1)}, u32[]{:S(2)}, u32[]{:S(2)}) collective-permute-start(bf16[128,128]{1,0:T(8,128)(2,1)S(1)} %get-tuple-element.23), channel_id=1, source_target_pairs={{0,8},{4,12},{8,0},{12,4},{1,9},{5,13},{9,1},{13,5},{2,10},{6,14},... | collective-permute-start | bytes 98312 | tf_op jit(solution)/shard_map/ppermute | solution.py:134
  12.8 0.3 %collective-permute-start.5 = (bf16[128,128]{1,0:T(8,128)(2,1)S(1)}, bf16[128,128]{1,0:T(8,128)(2,1)S(1)}, u32[]{:S(2)}, u32[]{:S(2)}) collective-permute-start(bf16[128,128]{1,0:T(8,128)(2,1)S(1)} %get-tuple-element.24), channel_id=1, source_target_pairs={{0,12},{4,8},{8,4},{12,0},{1,13},{5,9},{9,5},{13,1},{2,14},{6,10},... | collective-permute-start | bytes 98312 | tf_op jit(solution)/shard_map/ppermute | solution.py:134
  13.1 0.0 copy-done
  13.1 0.0 copy-start.1
  13.1 0.2 %near.1.near_ref = f32[128,128]{1,0:T(8,128)S(1)} custom-call(bf16[128,512]{1,0:T(8,128)(2,1)S(1)} %copy-done, bf16[512,128]{1,0:T(8,128)(2,1)S(1)} %get-tuple-element.21.rows_ref), custom_call_target="tpu_custom_call" | custom-call | flops 16777216 | tf_op jit(solution)/shard_map/near/pallas_call | solution.py:139
  13.3 0.0 collective-permute-done.3.refs_0_
  13.3 1.9 %collective-permute-done.4.refs_1_ = bf16[128,128]{1,0:T(8,128)(2,1)S(1)} collective-permute-done((bf16[128,128]{1,0:T(8,128)(2,1)S(1)}, bf16[128,128]{1,0:T(8,128)(2,1)S(1)}, u32[]{:S(2)}, u32[]{:S(2)}) %collective-permute-start.4) | collective-permute-done | bytes 32800 | tf_op jit(solution)/shard_map/ppermute | solution.py:134
  15.2 1.0 %collective-permute-done.5.refs_2_ = bf16[128,128]{1,0:T(8,128)(2,1)S(1)} collective-permute-done((bf16[128,128]{1,0:T(8,128)(2,1)S(1)}, bf16[128,128]{1,0:T(8,128)(2,1)S(1)}, u32[]{:S(2)}, u32[]{:S(2)}) %collective-permute-start.5) | collective-permute-done | bytes 32800 | tf_op jit(solution)/shard_map/ppermute | solution.py:134
  16.2 0.0 copy-done.1
  16.2 0.8 %finish.1 = f32[128,128]{1,0:T(8,128)} custom-call(f32[128,128]{1,0:T(8,128)S(1)} %get-tuple-element.15.mask_ref, f32[128,128]{1,0:T(8,128)S(1)} %near.1.near_ref, bf16[128,512]{1,0:T(8,128)(2,1)S(1)} %copy-done.1, bf16[128,128]{1,0:T(8,128)(2,1)S(1)} %collective-permute-done.3.refs_0_, bf16[128,128]{1,0:T(8,128)(2,1)S(1)} %collective-permute-done.4.refs_1_, ...), custom_call_target="tpu_custom_call" | custom-call | flops 16777216 | tf_op jit(solution)/shard_map/finish/pallas_call | solution.py:158
Async XLA Ops:
  0.9 7.6 %collective-permute-start = (bf16[224,128]{1,0:T(8,128)(2,1)S(1)}, bf16[224,128]{1,0:T(8,128)(2,1)S(1)}, u32[]{:S(2)}, u32[]{:S(2)}) collective-permute-start(bf16[224,128]{1,0:T(8,128)(2,1)S(1)} %get-tuple-element.18), channel_id=1, source_target_pairs={{0,1},{1,2},{2,3},{3,0},{4,5},{5,6},{6,7},{7,4},{8,9},{9,10},{10,1... | collective-permute-start | bytes 172040 | tf_op jit(solution)/shard_map/ppermute | solution.py:84
  4.0 3.9 %copy-start.2 = (s32[16]{0:T(128)S(1)}, s32[16]{0:T(128)}, u32[]{:S(2)}) copy-start(s32[16]{0:T(128)} %size_ref.1) | copy-start | bytes 196
  4.0 6.6 %collective-permute-start.1 = (bf16[224,128]{1,0:T(8,128)(2,1)S(1)}, bf16[224,128]{1,0:T(8,128)(2,1)S(1)}, u32[]{:S(2)}, u32[]{:S(2)}) collective-permute-start(bf16[224,128]{1,0:T(8,128)(2,1)S(1)} %get-tuple-element.19), channel_id=1, source_target_pairs={{0,2},{1,3},{2,0},{3,1},{4,6},{5,7},{6,4},{7,5},{8,10},{9,11},{10,... | collective-permute-start | bytes 172040 | tf_op jit(solution)/shard_map/ppermute | solution.py:84
  6.5 4.4 %collective-permute-start.2 = (bf16[224,128]{1,0:T(8,128)(2,1)S(1)}, bf16[224,128]{1,0:T(8,128)(2,1)S(1)}, u32[]{:S(2)}, u32[]{:S(2)}) collective-permute-start(bf16[224,128]{1,0:T(8,128)(2,1)S(1)} %get-tuple-element.20), channel_id=1, source_target_pairs={{0,3},{1,0},{2,1},{3,2},{4,7},{5,4},{6,5},{7,6},{8,11},{9,8},{10,9... | collective-permute-start | bytes 172040 | tf_op jit(solution)/shard_map/ppermute | solution.py:84
  11.0 2.1 %copy-start = (bf16[128,512]{1,0:T(8,128)(2,1)S(1)}, bf16[128,512]{1,0:T(8,128)(2,1)}, u32[]{:S(2)}) copy-start(bf16[128,512]{1,0:T(8,128)(2,1)} %block_ref.1) | copy-start | bytes 393220
  11.1 2.1 %collective-permute-start.3 = (bf16[128,128]{1,0:T(8,128)(2,1)S(1)}, bf16[128,128]{1,0:T(8,128)(2,1)S(1)}, u32[]{:S(2)}, u32[]{:S(2)}) collective-permute-start(bf16[128,128]{1,0:T(8,128)(2,1)S(1)} %get-tuple-element.22), channel_id=1, source_target_pairs={{0,4},{4,0},{8,12},{12,8},{1,5},{5,1},{9,13},{13,9},{2,6},{6,2},{1... | collective-permute-start | bytes 98312 | tf_op jit(solution)/shard_map/ppermute | solution.py:134
  11.2 4.0 %collective-permute-start.4 = (bf16[128,128]{1,0:T(8,128)(2,1)S(1)}, bf16[128,128]{1,0:T(8,128)(2,1)S(1)}, u32[]{:S(2)}, u32[]{:S(2)}) collective-permute-start(bf16[128,128]{1,0:T(8,128)(2,1)S(1)} %get-tuple-element.23), channel_id=1, source_target_pairs={{0,8},{4,12},{8,0},{12,4},{1,9},{5,13},{9,1},{13,5},{2,10},{6,14},... | collective-permute-start | bytes 98312 | tf_op jit(solution)/shard_map/ppermute | solution.py:134
  12.8 3.4 %collective-permute-start.5 = (bf16[128,128]{1,0:T(8,128)(2,1)S(1)}, bf16[128,128]{1,0:T(8,128)(2,1)S(1)}, u32[]{:S(2)}, u32[]{:S(2)}) collective-permute-start(bf16[128,128]{1,0:T(8,128)(2,1)S(1)} %get-tuple-element.24), channel_id=1, source_target_pairs={{0,12},{4,8},{8,4},{12,0},{1,13},{5,9},{9,5},{13,1},{2,14},{6,10},... | collective-permute-start | bytes 98312 | tf_op jit(solution)/shard_map/ppermute | solution.py:134
  13.1 3.1 %copy-start.1 = (bf16[128,512]{1,0:T(8,128)(2,1)S(1)}, bf16[128,512]{1,0:T(8,128)(2,1)}, u32[]{:S(2)}) copy-start(bf16[128,512]{1,0:T(8,128)(2,1)} %factor_ref.1) | copy-start | bytes 393220

commit v2 on v1

--- a/solution.py
+++ b/solution.py
@@ -105,66 +105,102 @@
         name="mask",
     )(cluster_size)
 
+    def weigh(step, mask_ref, parcel, outs):
+        sub = lax.axis_index("sub")
+        origin = behind(sub, step)
+        rows = parcel[0:slots, :] * mask_ref[at(origin * slots, slots), :]
+        part = jnp.dot(parcel[slots:, :], rows, preferred_element_type=f32).astype(bf16)
+        for hop in range(1, regions):
+            outs[hop - 1][at(origin * rank, rank), :] = part[(hop - 1) * rank : hop * rank, :]
+
     def regroup(mask_ref, *refs):
-        ins, outs, rows_ref = refs[:groups], refs[groups:-1], refs[-1]
-        sub = lax.axis_index("sub")
-        for step in range(groups):
-            origin = behind(sub, step)
-            here = at(origin * slots, slots)
-            rows = ins[step][0:slots, :] * mask_ref[here, :]
-            rows_ref[here, :] = rows
-            part = jnp.dot(ins[step][slots:, :], rows, preferred_element_type=f32).astype(bf16)
-            for hop in range(1, regions):
-                outs[hop - 1][at(origin * rank, rank), :] = part[(hop - 1) * rank : hop * rank, :]
-
-    *letters, group_rows = pl.pallas_call(
+        for step in range(groups - 1):
+            weigh(step, mask_ref, refs[step], refs[groups - 1 :])
+
+    def complete(mask_ref, parcel, *refs):
+        weigh(groups - 1, mask_ref, parcel, refs[regions - 1 :])
+
+    letter_shapes = [jax.ShapeDtypeStruct((height, loads), bf16)] * (regions - 1)
+    letters = pl.pallas_call(
         regroup,
-        out_shape=[jax.ShapeDtypeStruct((height, loads), bf16)] * (regions - 1)
-        + [jax.ShapeDtypeStruct((groups * slots, loads), bf16)],
-        in_specs=[VMEM] * (groups + 1),
-        out_specs=[VMEM] * regions,
+        out_shape=letter_shapes,
+        in_specs=[VMEM] * groups,
+        out_specs=[VMEM] * (regions - 1),
         compiler_params=PARAMS,
         cost_estimate=cost(1 << 20),
         name="regroup",
-    )(group_mask, *held)
+    )(group_mask, *held[:-1])
+    letters = pl.pallas_call(
+        complete,
+        out_shape=letter_shapes,
+        in_specs=[VMEM] * (regions + 1),
+        out_specs=[VMEM] * (regions - 1),
+        input_output_aliases={hop + 1: hop - 1 for hop in range(1, regions)},
+        compiler_params=PARAMS,
+        cost_estimate=cost(1 << 20),
+        name="complete",
+    )(group_mask, held[-1], *letters)
 
     received = {}
     for hop in hops:
         pairs = [(r, r ^ hop) for r in range(regions)]
         received[hop] = lax.ppermute(letters[hop - 1], "region", pairs)
 
-    def near(block_ref, rows_ref, out):
-        out[...] = jnp.dot(block_ref[...], rows_ref[...], preferred_element_type=f32)
+    late = min(2, regions - 1)
+    early = [hop for hop in range(1, regions) if hop != late]
+
+    def far_part(factor_ref, letter, hop):
+        start = across(lax.axis_index("region"), hop) * height
+        return jnp.dot(factor_ref[:, at(start, height)], letter[...], preferred_element_type=f32)
+
+    def near(block_ref, mask_ref, *refs):
+        parcels, out, stack = refs[:groups], refs[groups], refs[groups + 1]
+        sub = lax.axis_index("sub")
+        for step in range(groups):
+            here = at(behind(sub, step) * slots, slots)
+            stack[here, :] = parcels[step][0:slots, :] * mask_ref[here, :]
+        out[...] = jnp.dot(block_ref[...], stack[...], preferred_element_type=f32)
 
     near_sum = pl.pallas_call(
         near,
         out_shape=jax.ShapeDtypeStruct((slots, loads), f32),
-        in_specs=[VMEM] * 2,
+        in_specs=[VMEM] * (groups + 2),
         out_specs=VMEM,
+        scratch_shapes=[pltpu.VMEM((groups * slots, loads), bf16)],
         compiler_params=PARAMS,
         cost_estimate=cost(1 << 24),
         name="near",
-    )(near_block, group_rows)
-
-    def finish(mask_ref, near_ref, factor_ref, *refs):
-        ins, out, scratch = refs[: regions - 1], refs[regions - 1], refs[regions]
-        region = lax.axis_index("region")
-        scratch[at(region * height, height), :] = jnp.zeros((height, loads), bf16)
-        for hop in range(1, regions):
-            scratch[at(across(region, hop) * height, height), :] = ins[hop - 1][...]
-        far = jnp.dot(factor_ref[...], scratch[...], preferred_element_type=f32)
-        out[...] = jnp.where(mask_ref[...] > 0.0, near_ref[...] + far, 0.0)
+    )(near_block, group_mask, *held)
+
+    def gain(near_ref, factor_ref, *refs):
+        total = near_ref[...]
+        for hop, letter in zip(early, refs):
+            total += far_part(factor_ref, letter, hop)
+        refs[-1][...] = total
+
+    partial = pl.pallas_call(
+        gain,
+        out_shape=jax.ShapeDtypeStruct((slots, loads), f32),
+        in_specs=[VMEM] * (len(early) + 2),
+        out_specs=VMEM,
+        compiler_params=PARAMS,
+        cost_estimate=cost(1 << 24),
+        name="gain",
+    )(near_sum, row_factor, *(received[hop] for hop in early))
+
+    def finish(mask_ref, partial_ref, factor_ref, letter, out):
+        total = partial_ref[...] + far_part(factor_ref, letter, late)
+        out[...] = jnp.where(mask_ref[...] > 0.0, total, 0.0)
 
     return pl.pallas_call(
         finish,
         out_shape=jax.ShapeDtypeStruct((slots, loads), f32),
-        in_specs=[VMEM] * (regions + 2),
+        in_specs=[VMEM] * 4,
         out_specs=VMEM,
-        scratch_shapes=[pltpu.VMEM((clusters * rank, loads), bf16)],
         compiler_params=PARAMS,
         cost_estimate=cost(1 << 24),
         name="finish",
-    )(own_mask, near_sum, row_factor, *(received[hop] for hop in range(1, regions)))
+    )(own_mask, partial, row_factor, received[late])
 
 
 def solution(mesh):

time: 17.2 us -> 17.7 us (1.029)
  Pallas kernels: 2.61 us -> 2.88 us
  starting transfers between devices: 8.96 us -> 9.19 us
    pallas_call x1 -> x3, Pallas kernels: 0.18 us -> 0.46 us  [the longest x1 0.18 us: local(): pl.pallas_call(regroup, out_shape=letter_shapes, in_specs=[VMEM] * groups...]
    ppermute x3, starting transfers between devices: 1.92 us -> 2.15 us  [local(): received[hop] = lax.ppermute(letters[hop - 1], 'region', pairs)]
    ppermute x3, waiting for transfers between devices: 2.45 us -> 2.26 us  [local(): held.append(lax.ppermute(parcels[step], 'sub', pairs))]
  transfers between devices with their start and end apart: 6 -> 6, of which waited for: 4 -> 4; matrix products, arithmetic and copies ran while one was open for 0% -> 0% of each run, Pallas kernels for 4% -> 6%
where the time goes in v2:
time: 17.7 us; the launch traced here: 17.5 us
  starting transfers between devices  9.19 us (52%)
  waiting for transfers between devices  5.33 us (30%)
  Pallas kernels  2.88 us (16%)
    ppermute x3, starting transfers between devices, local(): held.append(lax.ppermute(parcels[step], 'sub', pairs))  7.04 us
    ppermute x3, waiting for transfers between devices, local(): received[hop] = lax.ppermute(letters[hop - 1], 'region', pairs)  3.07 us
    ppermute x3, waiting for transfers between devices, local(): held.append(lax.ppermute(parcels[step], 'sub', pairs))  2.26 us
    ppermute x3, starting transfers between devices, local(): received[hop] = lax.ppermute(letters[hop - 1], 'region', pairs)  2.15 us
    pallas_call x1, Pallas kernels, local(): pl.pallas_call(gather, out_shape=[jax.ShapeDtypeStruct((slots + width, lo...  0.84 us
    pallas_call x1, Pallas kernels, local(): pl.pallas_call(finish, out_shape=jax.ShapeDtypeStruct((slots, loads), f32...  0.77 us
    pallas_call x1, Pallas kernels, local(): pl.pallas_call(mask, out_shape=[jax.ShapeDtypeStruct((groups * slots, loa...  0.59 us
  transfers between devices with their start and end apart: 6, of which 4 were waited for; matrix products, arithmetic and copies ran while one was open for 0% of the time, Pallas kernels for 6%

profile of v2, /device:TPU:0, one launch (start us, length us, event | category | flops | bytes accessed | tf_op | source)
XLA Modules:
  0.0 17.5 jit_solution(5154651854757121533)
XLA Ops:
  0.0 0.8 %gather.1 = (bf16[224,128]{1,0:T(8,128)(2,1)S(1)}, bf16[224,128]{1,0:T(8,128)(2,1)S(1)}, bf16[224,128]{1,0:T(8,128)(2,1)S(1)}, bf16[224,128]{1,0:T(8,128)(2,1)S(1)}) custom-call(bf16[128,128]{1,0:T(8,128)(2,1)} %dens.1, bf16[4,4,32,128]{3,2,1,0:T(8,128)(2,1)} %bitcast.1), custom_call_target="tpu_custom_call" | custom-call | tf_op jit(solution)/shard_map/gather/pallas_call | solution.py:64
  0.9 3.1 %collective-permute-start = (bf16[224,128]{1,0:T(8,128)(2,1)S(1)}, bf16[224,128]{1,0:T(8,128)(2,1)S(1)}, u32[]{:S(2)}, u32[]{:S(2)}) collective-permute-start(bf16[224,128]{1,0:T(8,128)(2,1)S(1)} %get-tuple-element.20), channel_id=1, source_target_pairs={{0,1},{1,2},{2,3},{3,0},{4,5},{5,6},{6,7},{7,4},{8,9},{9,10},{10,1... | collective-permute-start | bytes 172040 | tf_op jit(solution)/shard_map/ppermute | solution.py:84
  4.0 0.0 copy-start.2
  4.0 2.6 %collective-permute-start.1 = (bf16[224,128]{1,0:T(8,128)(2,1)S(1)}, bf16[224,128]{1,0:T(8,128)(2,1)S(1)}, u32[]{:S(2)}, u32[]{:S(2)}) collective-permute-start(bf16[224,128]{1,0:T(8,128)(2,1)S(1)} %get-tuple-element.21), channel_id=1, source_target_pairs={{0,2},{1,3},{2,0},{3,1},{4,6},{5,7},{6,4},{7,5},{8,10},{9,11},{10,... | collective-permute-start | bytes 172040 | tf_op jit(solution)/shard_map/ppermute | solution.py:84
  6.5 1.3 %collective-permute-start.2 = (bf16[224,128]{1,0:T(8,128)(2,1)S(1)}, bf16[224,128]{1,0:T(8,128)(2,1)S(1)}, u32[]{:S(2)}, u32[]{:S(2)}) collective-permute-start(bf16[224,128]{1,0:T(8,128)(2,1)S(1)} %get-tuple-element.22), channel_id=1, source_target_pairs={{0,3},{1,0},{2,1},{3,2},{4,7},{5,4},{6,5},{7,6},{8,11},{9,8},{10,9... | collective-permute-start | bytes 172040 | tf_op jit(solution)/shard_map/ppermute | solution.py:84
  7.9 0.0 copy-done.2
  7.9 0.6 %mask.1 = (bf16[512,128]{1,0:T(8,128)(2,1)S(1)}, f32[128,128]{1,0:T(8,128)S(1)}) custom-call(s32[16]{0:T(128)S(1)} %copy-done.2), custom_call_target="tpu_custom_call" | custom-call | flops 1048576 | tf_op jit(solution)/shard_map/mask/pallas_call | solution.py:95
  8.5 0.0 collective-permute-done.refs_1_
  8.5 2.1 %collective-permute-done.1.refs_2_ = bf16[224,128]{1,0:T(8,128)(2,1)S(1)} collective-permute-done((bf16[224,128]{1,0:T(8,128)(2,1)S(1)}, bf16[224,128]{1,0:T(8,128)(2,1)S(1)}, u32[]{:S(2)}, u32[]{:S(2)}) %collective-permute-start.1) | collective-permute-done | bytes 57376 | tf_op jit(solution)/shard_map/ppermute | solution.py:84
  10.6 0.2 %regroup.1 = (bf16[128,128]{1,0:T(8,128)(2,1)S(1)}, bf16[128,128]{1,0:T(8,128)(2,1)S(1)}, bf16[128,128]{1,0:T(8,128)(2,1)S(1)}) custom-call(bf16[512,128]{1,0:T(8,128)(2,1)S(1)} %get-tuple-element.18.mask_ref, bf16[224,128]{1,0:T(8,128)(2,1)S(1)} %get-tuple-element.19.refs_0_, bf16[224,128]{1,0:T(8,128)(2,1)S(1)} %collective-permute-done.refs_1_, ...), custom_call_target="tpu_custom_call" | custom-call | flops 1048576 | tf_op jit(solution)/shard_map/regroup/pallas_call | solution.py:124
  10.8 0.2 collective-permute-done.2.refs_3_.parcel
  11.0 0.0 copy-start.1
  11.0 0.1 complete.1
  11.1 0.0 collective-permute-start.3
  11.1 1.7 %collective-permute-start.4 = (bf16[128,128]{1,0:T(8,128)(2,1)S(1)}, bf16[128,128]{1,0:T(8,128)(2,1)S(1)}, u32[]{:S(2)}, u32[]{:S(2)}) collective-permute-start(bf16[128,128]{1,0:T(8,128)(2,1)S(1)} %get-tuple-element.27), channel_id=1, source_target_pairs={{0,12},{4,8},{8,4},{12,0},{1,13},{5,9},{9,5},{13,1},{2,14},{6,10},... | collective-permute-start | bytes 98312 | tf_op jit(solution)/shard_map/ppermute | solution.py:147
  12.8 0.0 copy-start
  12.8 0.5 %collective-permute-start.5 = (bf16[128,128]{1,0:T(8,128)(2,1)S(1)}, bf16[128,128]{1,0:T(8,128)(2,1)S(1)}, u32[]{:S(2)}, u32[]{:S(2)}) collective-permute-start(bf16[128,128]{1,0:T(8,128)(2,1)S(1)} %get-tuple-element.28), channel_id=1, source_target_pairs={{0,8},{4,12},{8,0},{12,4},{1,9},{5,13},{9,1},{13,5},{2,10},{6,14},... | collective-permute-start | bytes 98312 | tf_op jit(solution)/shard_map/ppermute | solution.py:147
  13.2 0.0 copy-done.1
  13.2 0.2 %near.1.near_ref = f32[128,128]{1,0:T(8,128)S(1)} custom-call(bf16[128,512]{1,0:T(8,128)(2,1)S(1)} %copy-done.1, bf16[512,128]{1,0:T(8,128)(2,1)S(1)} %get-tuple-element.18.mask_ref, bf16[224,128]{1,0:T(8,128)(2,1)S(1)} %get-tuple-element.19.refs_0_, bf16[224,128]{1,0:T(8,128)(2,1)S(1)} %collective-permute-done.refs_1_, ...), custom_call_target="tpu_custom_call" | custom-call | flops 16777216 | tf_op jit(solution)/shard_map/near/pallas_call | solution.py:164
  13.5 0.0 collective-permute-done.3.refs_0_
  13.5 1.0 %collective-permute-done.4.refs_1_ = bf16[128,128]{1,0:T(8,128)(2,1)S(1)} collective-permute-done((bf16[128,128]{1,0:T(8,128)(2,1)S(1)}, bf16[128,128]{1,0:T(8,128)(2,1)S(1)}, u32[]{:S(2)}, u32[]{:S(2)}) %collective-permute-start.4) | collective-permute-done | bytes 32800 | tf_op jit(solution)/shard_map/ppermute | solution.py:147
  14.5 0.0 copy-done
  14.5 0.2 gain.1.partial_ref
  14.7 2.0 %collective-permute-done.5.letter = bf16[128,128]{1,0:T(8,128)(2,1)S(1)} collective-permute-done((bf16[128,128]{1,0:T(8,128)(2,1)S(1)}, bf16[128,128]{1,0:T(8,128)(2,1)S(1)}, u32[]{:S(2)}, u32[]{:S(2)}) %collective-permute-start.5) | collective-permute-done | bytes 32800 | tf_op jit(solution)/shard_map/ppermute | solution.py:147
  16.7 0.8 %finish.1 = f32[128,128]{1,0:T(8,128)} custom-call(f32[128,128]{1,0:T(8,128)S(1)} %get-tuple-element.17.mask_ref, f32[128,128]{1,0:T(8,128)S(1)} %gain.1.partial_ref, bf16[128,512]{1,0:T(8,128)(2,1)S(1)} %copy-done, bf16[128,128]{1,0:T(8,128)(2,1)S(1)} %collective-permute-done.5.letter), custom_call_target="tpu_custom_call" | custom-call | flops 16777216 | tf_op jit(solution)/shard_map/finish/pallas_call | solution.py:195
Async XLA Ops:
  0.9 7.6 %collective-permute-start = (bf16[224,128]{1,0:T(8,128)(2,1)S(1)}, bf16[224,128]{1,0:T(8,128)(2,1)S(1)}, u32[]{:S(2)}, u32[]{:S(2)}) collective-permute-start(bf16[224,128]{1,0:T(8,128)(2,1)S(1)} %get-tuple-element.20), channel_id=1, source_target_pairs={{0,1},{1,2},{2,3},{3,0},{4,5},{5,6},{6,7},{7,4},{8,9},{9,10},{10,1... | collective-permute-start | bytes 172040 | tf_op jit(solution)/shard_map/ppermute | solution.py:84
  4.0 3.9 %copy-start.2 = (s32[16]{0:T(128)S(1)}, s32[16]{0:T(128)}, u32[]{:S(2)}) copy-start(s32[16]{0:T(128)} %size_ref.1) | copy-start | bytes 196
  4.0 6.6 %collective-permute-start.1 = (bf16[224,128]{1,0:T(8,128)(2,1)S(1)}, bf16[224,128]{1,0:T(8,128)(2,1)S(1)}, u32[]{:S(2)}, u32[]{:S(2)}) collective-permute-start(bf16[224,128]{1,0:T(8,128)(2,1)S(1)} %get-tuple-element.21), channel_id=1, source_target_pairs={{0,2},{1,3},{2,0},{3,1},{4,6},{5,7},{6,4},{7,5},{8,10},{9,11},{10,... | collective-permute-start | bytes 172040 | tf_op jit(solution)/shard_map/ppermute | solution.py:84
  6.5 4.4 %collective-permute-start.2 = (bf16[224,128]{1,0:T(8,128)(2,1)S(1)}, bf16[224,128]{1,0:T(8,128)(2,1)S(1)}, u32[]{:S(2)}, u32[]{:S(2)}) collective-permute-start(bf16[224,128]{1,0:T(8,128)(2,1)S(1)} %get-tuple-element.22), channel_id=1, source_target_pairs={{0,3},{1,0},{2,1},{3,2},{4,7},{5,4},{6,5},{7,6},{8,11},{9,8},{10,9... | collective-permute-start | bytes 172040 | tf_op jit(solution)/shard_map/ppermute | solution.py:84
  11.0 2.3 %copy-start.1 = (bf16[128,512]{1,0:T(8,128)(2,1)S(1)}, bf16[128,512]{1,0:T(8,128)(2,1)}, u32[]{:S(2)}) copy-start(bf16[128,512]{1,0:T(8,128)(2,1)} %block_ref.1) | copy-start | bytes 393220
  11.1 2.4 %collective-permute-start.3 = (bf16[128,128]{1,0:T(8,128)(2,1)S(1)}, bf16[128,128]{1,0:T(8,128)(2,1)S(1)}, u32[]{:S(2)}, u32[]{:S(2)}) collective-permute-start(bf16[128,128]{1,0:T(8,128)(2,1)S(1)} %get-tuple-element.26), channel_id=1, source_target_pairs={{0,4},{4,0},{8,12},{12,8},{1,5},{5,1},{9,13},{13,9},{2,6},{6,2},{1... | collective-permute-start | bytes 98312 | tf_op jit(solution)/shard_map/ppermute | solution.py:147
  11.1 3.4 %collective-permute-start.4 = (bf16[128,128]{1,0:T(8,128)(2,1)S(1)}, bf16[128,128]{1,0:T(8,128)(2,1)S(1)}, u32[]{:S(2)}, u32[]{:S(2)}) collective-permute-start(bf16[128,128]{1,0:T(8,128)(2,1)S(1)} %get-tuple-element.27), channel_id=1, source_target_pairs={{0,12},{4,8},{8,4},{12,0},{1,13},{5,9},{9,5},{13,1},{2,14},{6,10},... | collective-permute-start | bytes 98312 | tf_op jit(solution)/shard_map/ppermute | solution.py:147
  12.8 1.7 %copy-start = (bf16[128,512]{1,0:T(8,128)(2,1)S(1)}, bf16[128,512]{1,0:T(8,128)(2,1)}, u32[]{:S(2)}) copy-start(bf16[128,512]{1,0:T(8,128)(2,1)} %factor_ref.3) | copy-start | bytes 393220
  12.8 3.9 %collective-permute-start.5 = (bf16[128,128]{1,0:T(8,128)(2,1)S(1)}, bf16[128,128]{1,0:T(8,128)(2,1)S(1)}, u32[]{:S(2)}, u32[]{:S(2)}) collective-permute-start(bf16[128,128]{1,0:T(8,128)(2,1)S(1)} %get-tuple-element.28), channel_id=1, source_target_pairs={{0,8},{4,12},{8,0},{12,4},{1,9},{5,13},{9,1},{13,5},{2,10},{6,14},... | collective-permute-start | bytes 98312 | tf_op jit(solution)/shard_map/ppermute | solution.py:147

commit v3 on v2

--- a/solution.py
+++ b/solution.py
@@ -118,7 +118,10 @@
             weigh(step, mask_ref, refs[step], refs[groups - 1 :])
 
     def complete(mask_ref, parcel, *refs):
-        weigh(groups - 1, mask_ref, parcel, refs[regions - 1 :])
+        begun, outs = refs[: regions - 1], refs[regions - 1 :]
+        for source, out in zip(begun, outs):
+            out[...] = source[...]
+        weigh(groups - 1, mask_ref, parcel, outs)
 
     letter_shapes = [jax.ShapeDtypeStruct((height, loads), bf16)] * (regions - 1)
     letters = pl.pallas_call(
@@ -135,7 +138,6 @@
         out_shape=letter_shapes,
         in_specs=[VMEM] * (regions + 1),
         out_specs=[VMEM] * (regions - 1),
-        input_output_aliases={hop + 1: hop - 1 for hop in range(1, regions)},
         compiler_params=PARAMS,
         cost_estimate=cost(1 << 20),
         name="complete",

time: 17.7 us -> 17.7 us (level)
  no operation moved by 1% of the time
where the time goes in v3:
time: 17.7 us; the launch traced here: 17.5 us
  starting transfers between devices  9.19 us (52%)
  waiting for transfers between devices  5.33 us (30%)
  Pallas kernels  2.88 us (16%)
    ppermute x3, starting transfers between devices, local(): held.append(lax.ppermute(parcels[step], 'sub', pairs))  7.04 us
    ppermute x3, waiting for transfers between devices, local(): received[hop] = lax.ppermute(letters[hop - 1], 'region', pairs)  3.07 us
    ppermute x3, waiting for transfers between devices, local(): held.append(lax.ppermute(parcels[step], 'sub', pairs))  2.26 us
    ppermute x3, starting transfers between devices, local(): received[hop] = lax.ppermute(letters[hop - 1], 'region', pairs)  2.14 us
    pallas_call x1, Pallas kernels, local(): pl.pallas_call(gather, out_shape=[jax.ShapeDtypeStruct((slots + width, lo...  0.84 us
    pallas_call x1, Pallas kernels, local(): pl.pallas_call(finish, out_shape=jax.ShapeDtypeStruct((slots, loads), f32...  0.77 us
    pallas_call x1, Pallas kernels, local(): pl.pallas_call(mask, out_shape=[jax.ShapeDtypeStruct((groups * slots, loa...  0.59 us
  transfers between devices with their start and end apart: 6, of which 4 were waited for; matrix products, arithmetic and copies ran while one was open for 0% of the time, Pallas kernels for 6%

profile of v3, /device:TPU:0, one launch (start us, length us, event | category | flops | bytes accessed | tf_op | source)
XLA Modules:
  0.0 17.5 jit_solution(1215406091815723590)
XLA Ops:
  0.0 0.8 %gather.1 = (bf16[224,128]{1,0:T(8,128)(2,1)S(1)}, bf16[224,128]{1,0:T(8,128)(2,1)S(1)}, bf16[224,128]{1,0:T(8,128)(2,1)S(1)}, bf16[224,128]{1,0:T(8,128)(2,1)S(1)}) custom-call(bf16[128,128]{1,0:T(8,128)(2,1)} %dens.1, bf16[4,4,32,128]{3,2,1,0:T(8,128)(2,1)} %bitcast.1), custom_call_target="tpu_custom_call" | custom-call | tf_op jit(solution)/shard_map/gather/pallas_call | solution.py:64
  0.9 3.1 %collective-permute-start = (bf16[224,128]{1,0:T(8,128)(2,1)S(1)}, bf16[224,128]{1,0:T(8,128)(2,1)S(1)}, u32[]{:S(2)}, u32[]{:S(2)}) collective-permute-start(bf16[224,128]{1,0:T(8,128)(2,1)S(1)} %get-tuple-element.20), channel_id=1, source_target_pairs={{0,1},{1,2},{2,3},{3,0},{4,5},{5,6},{6,7},{7,4},{8,9},{9,10},{10,1... | collective-permute-start | bytes 172040 | tf_op jit(solution)/shard_map/ppermute | solution.py:84
  4.0 0.0 copy-start.2
  4.0 2.6 %collective-permute-start.1 = (bf16[224,128]{1,0:T(8,128)(2,1)S(1)}, bf16[224,128]{1,0:T(8,128)(2,1)S(1)}, u32[]{:S(2)}, u32[]{:S(2)}) collective-permute-start(bf16[224,128]{1,0:T(8,128)(2,1)S(1)} %get-tuple-element.21), channel_id=1, source_target_pairs={{0,2},{1,3},{2,0},{3,1},{4,6},{5,7},{6,4},{7,5},{8,10},{9,11},{10,... | collective-permute-start | bytes 172040 | tf_op jit(solution)/shard_map/ppermute | solution.py:84
  6.5 1.3 %collective-permute-start.2 = (bf16[224,128]{1,0:T(8,128)(2,1)S(1)}, bf16[224,128]{1,0:T(8,128)(2,1)S(1)}, u32[]{:S(2)}, u32[]{:S(2)}) collective-permute-start(bf16[224,128]{1,0:T(8,128)(2,1)S(1)} %get-tuple-element.22), channel_id=1, source_target_pairs={{0,3},{1,0},{2,1},{3,2},{4,7},{5,4},{6,5},{7,6},{8,11},{9,8},{10,9... | collective-permute-start | bytes 172040 | tf_op jit(solution)/shard_map/ppermute | solution.py:84
  7.9 0.0 copy-done.2
  7.9 0.6 %mask.1 = (bf16[512,128]{1,0:T(8,128)(2,1)S(1)}, f32[128,128]{1,0:T(8,128)S(1)}) custom-call(s32[16]{0:T(128)S(1)} %copy-done.2), custom_call_target="tpu_custom_call" | custom-call | flops 1048576 | tf_op jit(solution)/shard_map/mask/pallas_call | solution.py:95
  8.5 0.0 collective-permute-done.refs_1_
  8.5 2.1 %collective-permute-done.1.refs_2_ = bf16[224,128]{1,0:T(8,128)(2,1)S(1)} collective-permute-done((bf16[224,128]{1,0:T(8,128)(2,1)S(1)}, bf16[224,128]{1,0:T(8,128)(2,1)S(1)}, u32[]{:S(2)}, u32[]{:S(2)}) %collective-permute-start.1) | collective-permute-done | bytes 57376 | tf_op jit(solution)/shard_map/ppermute | solution.py:84
  10.6 0.2 %regroup.1 = (bf16[128,128]{1,0:T(8,128)(2,1)S(1)}, bf16[128,128]{1,0:T(8,128)(2,1)S(1)}, bf16[128,128]{1,0:T(8,128)(2,1)S(1)}) custom-call(bf16[512,128]{1,0:T(8,128)(2,1)S(1)} %get-tuple-element.18.mask_ref, bf16[224,128]{1,0:T(8,128)(2,1)S(1)} %get-tuple-element.19.refs_0_, bf16[224,128]{1,0:T(8,128)(2,1)S(1)} %collective-permute-done.refs_1_, ...), custom_call_target="tpu_custom_call" | custom-call | flops 1048576 | tf_op jit(solution)/shard_map/regroup/pallas_call | solution.py:127
  10.8 0.2 collective-permute-done.2.refs_3_.parcel
  11.0 0.0 copy-start.1
  11.0 0.1 complete.1
  11.1 0.0 collective-permute-start.3
  11.1 1.7 %collective-permute-start.4 = (bf16[128,128]{1,0:T(8,128)(2,1)S(1)}, bf16[128,128]{1,0:T(8,128)(2,1)S(1)}, u32[]{:S(2)}, u32[]{:S(2)}) collective-permute-start(bf16[128,128]{1,0:T(8,128)(2,1)S(1)} %get-tuple-element.27), channel_id=1, source_target_pairs={{0,12},{4,8},{8,4},{12,0},{1,13},{5,9},{9,5},{13,1},{2,14},{6,10},... | collective-permute-start | bytes 98312 | tf_op jit(solution)/shard_map/ppermute | solution.py:149
  12.8 0.0 copy-start
  12.8 0.5 %collective-permute-start.5 = (bf16[128,128]{1,0:T(8,128)(2,1)S(1)}, bf16[128,128]{1,0:T(8,128)(2,1)S(1)}, u32[]{:S(2)}, u32[]{:S(2)}) collective-permute-start(bf16[128,128]{1,0:T(8,128)(2,1)S(1)} %get-tuple-element.28), channel_id=1, source_target_pairs={{0,8},{4,12},{8,0},{12,4},{1,9},{5,13},{9,1},{13,5},{2,10},{6,14},... | collective-permute-start | bytes 98312 | tf_op jit(solution)/shard_map/ppermute | solution.py:149
  13.2 0.0 copy-done.1
  13.2 0.2 %near.1.near_ref = f32[128,128]{1,0:T(8,128)S(1)} custom-call(bf16[128,512]{1,0:T(8,128)(2,1)S(1)} %copy-done.1, bf16[512,128]{1,0:T(8,128)(2,1)S(1)} %get-tuple-element.18.mask_ref, bf16[224,128]{1,0:T(8,128)(2,1)S(1)} %get-tuple-element.19.refs_0_, bf16[224,128]{1,0:T(8,128)(2,1)S(1)} %collective-permute-done.refs_1_, ...), custom_call_target="tpu_custom_call" | custom-call | flops 16777216 | tf_op jit(solution)/shard_map/near/pallas_call | solution.py:166
  13.5 0.0 collective-permute-done.3.refs_0_
  13.5 1.0 %collective-permute-done.4.refs_1_ = bf16[128,128]{1,0:T(8,128)(2,1)S(1)} collective-permute-done((bf16[128,128]{1,0:T(8,128)(2,1)S(1)}, bf16[128,128]{1,0:T(8,128)(2,1)S(1)}, u32[]{:S(2)}, u32[]{:S(2)}) %collective-permute-start.4) | collective-permute-done | bytes 32800 | tf_op jit(solution)/shard_map/ppermute | solution.py:149
  14.5 0.0 copy-done
  14.5 0.2 gain.1.partial_ref
  14.7 2.0 %collective-permute-done.5.letter = bf16[128,128]{1,0:T(8,128)(2,1)S(1)} collective-permute-done((bf16[128,128]{1,0:T(8,128)(2,1)S(1)}, bf16[128,128]{1,0:T(8,128)(2,1)S(1)}, u32[]{:S(2)}, u32[]{:S(2)}) %collective-permute-start.5) | collective-permute-done | bytes 32800 | tf_op jit(solution)/shard_map/ppermute | solution.py:149
  16.7 0.8 %finish.1 = f32[128,128]{1,0:T(8,128)} custom-call(f32[128,128]{1,0:T(8,128)S(1)} %get-tuple-element.17.mask_ref, f32[128,128]{1,0:T(8,128)S(1)} %gain.1.partial_ref, bf16[128,512]{1,0:T(8,128)(2,1)S(1)} %copy-done, bf16[128,128]{1,0:T(8,128)(2,1)S(1)} %collective-permute-done.5.letter), custom_call_target="tpu_custom_call" | custom-call | flops 16777216 | tf_op jit(solution)/shard_map/finish/pallas_call | solution.py:197
Async XLA Ops:
  0.9 7.6 %collective-permute-start = (bf16[224,128]{1,0:T(8,128)(2,1)S(1)}, bf16[224,128]{1,0:T(8,128)(2,1)S(1)}, u32[]{:S(2)}, u32[]{:S(2)}) collective-permute-start(bf16[224,128]{1,0:T(8,128)(2,1)S(1)} %get-tuple-element.20), channel_id=1, source_target_pairs={{0,1},{1,2},{2,3},{3,0},{4,5},{5,6},{6,7},{7,4},{8,9},{9,10},{10,1... | collective-permute-start | bytes 172040 | tf_op jit(solution)/shard_map/ppermute | solution.py:84
  4.0 3.9 %copy-start.2 = (s32[16]{0:T(128)S(1)}, s32[16]{0:T(128)}, u32[]{:S(2)}) copy-start(s32[16]{0:T(128)} %size_ref.1) | copy-start | bytes 196
  4.0 6.6 %collective-permute-start.1 = (bf16[224,128]{1,0:T(8,128)(2,1)S(1)}, bf16[224,128]{1,0:T(8,128)(2,1)S(1)}, u32[]{:S(2)}, u32[]{:S(2)}) collective-permute-start(bf16[224,128]{1,0:T(8,128)(2,1)S(1)} %get-tuple-element.21), channel_id=1, source_target_pairs={{0,2},{1,3},{2,0},{3,1},{4,6},{5,7},{6,4},{7,5},{8,10},{9,11},{10,... | collective-permute-start | bytes 172040 | tf_op jit(solution)/shard_map/ppermute | solution.py:84
  6.5 4.4 %collective-permute-start.2 = (bf16[224,128]{1,0:T(8,128)(2,1)S(1)}, bf16[224,128]{1,0:T(8,128)(2,1)S(1)}, u32[]{:S(2)}, u32[]{:S(2)}) collective-permute-start(bf16[224,128]{1,0:T(8,128)(2,1)S(1)} %get-tuple-element.22), channel_id=1, source_target_pairs={{0,3},{1,0},{2,1},{3,2},{4,7},{5,4},{6,5},{7,6},{8,11},{9,8},{10,9... | collective-permute-start | bytes 172040 | tf_op jit(solution)/shard_map/ppermute | solution.py:84
  11.0 2.3 %copy-start.1 = (bf16[128,512]{1,0:T(8,128)(2,1)S(1)}, bf16[128,512]{1,0:T(8,128)(2,1)}, u32[]{:S(2)}) copy-start(bf16[128,512]{1,0:T(8,128)(2,1)} %block_ref.1) | copy-start | bytes 393220
  11.1 2.4 %collective-permute-start.3 = (bf16[128,128]{1,0:T(8,128)(2,1)S(1)}, bf16[128,128]{1,0:T(8,128)(2,1)S(1)}, u32[]{:S(2)}, u32[]{:S(2)}) collective-permute-start(bf16[128,128]{1,0:T(8,128)(2,1)S(1)} %get-tuple-element.26), channel_id=1, source_target_pairs={{0,4},{4,0},{8,12},{12,8},{1,5},{5,1},{9,13},{13,9},{2,6},{6,2},{1... | collective-permute-start | bytes 98312 | tf_op jit(solution)/shard_map/ppermute | solution.py:149
  11.1 3.4 %collective-permute-start.4 = (bf16[128,128]{1,0:T(8,128)(2,1)S(1)}, bf16[128,128]{1,0:T(8,128)(2,1)S(1)}, u32[]{:S(2)}, u32[]{:S(2)}) collective-permute-start(bf16[128,128]{1,0:T(8,128)(2,1)S(1)} %get-tuple-element.27), channel_id=1, source_target_pairs={{0,12},{4,8},{8,4},{12,0},{1,13},{5,9},{9,5},{13,1},{2,14},{6,10},... | collective-permute-start | bytes 98312 | tf_op jit(solution)/shard_map/ppermute | solution.py:149
  12.8 1.7 %copy-start = (bf16[128,512]{1,0:T(8,128)(2,1)S(1)}, bf16[128,512]{1,0:T(8,128)(2,1)}, u32[]{:S(2)}) copy-start(bf16[128,512]{1,0:T(8,128)(2,1)} %factor_ref.3) | copy-start | bytes 393220
  12.8 3.9 %collective-permute-start.5 = (bf16[128,128]{1,0:T(8,128)(2,1)S(1)}, bf16[128,128]{1,0:T(8,128)(2,1)S(1)}, u32[]{:S(2)}, u32[]{:S(2)}) collective-permute-start(bf16[128,128]{1,0:T(8,128)(2,1)S(1)} %get-tuple-element.28), channel_id=1, source_target_pairs={{0,8},{4,12},{8,0},{12,4},{1,9},{5,13},{9,1},{13,5},{2,10},{6,14},... | collective-permute-start | bytes 98312 | tf_op jit(solution)/shard_map/ppermute | solution.py:149

commit v4 on v2

v4 whole, which is shorter than its diff:
```python
import jax
import jax.numpy as jnp
from jax import lax
from jax.experimental import pallas as pl
from jax.experimental.pallas import tpu as pltpu
from jax.sharding import PartitionSpec as P


VMEM = pl.BlockSpec(memory_space=pltpu.VMEM)
HBM = pl.BlockSpec(memory_space=pltpu.HBM)
SMEM = pl.BlockSpec(memory_space=pltpu.SMEM)
PARAMS = pltpu.CompilerParams(vmem_limit_bytes=8 << 20)


def cost(flops):
    return pl.CostEstimate(flops=flops, bytes_accessed=0, transcendentals=0)


def folded(count):
    odd = list(range(1, count, 2))
    even = list(range(2, count, 2))
    return [0] + odd + even[::-1]


def at(start, size):
    return pl.ds(pl.multiple_of(start, size), size)


def local(densities, cluster_size, near_block, row_factor, column_factor):
    slots, loads = densities.shape
    groups = lax.axis_size("sub")
    regions = lax.axis_size("region")
    clusters = groups * regions
    rank = row_factor.shape[1] // clusters
    height = groups * rank
    width = (regions - 1) * rank
    bf16, f32 = jnp.bfloat16, jnp.float32
    hops = range(regions - 1, 0, -1)

    def ahead(sub, step):
        return lax.rem(sub + step, groups)

    def behind(sub, step):
        return lax.rem(sub + groups - step, groups)

    def across(region, hop):
        return lax.bitwise_xor(region, jnp.int32(hop))

    def pack(size_hbm, dens_hbm, col_hbm, *refs):
        outs, (size, dens, col, found, sems) = refs[:groups], refs[groups:]
        copies = [
            pltpu.make_async_copy(source, target, sems.at[i])
            for i, (source, target) in enumerate(((size_hbm, size), (dens_hbm, dens), (col_hbm, col)))
        ]
        for copy in copies:
            copy.start()
        sub = lax.axis_index("sub")
        region = lax.axis_index("region")
        slot = lax.broadcasted_iota(jnp.int32, (slots, loads), 0)
        for copy in copies[:2]:
            copy.wait()
        rows = dens[...] * jnp.where(slot < size[region * groups + sub], 1.0, 0.0).astype(bf16)
        copies[2].wait()
        for step in range(groups):
            goal = ahead(sub, step)
            for hop in range(1, regions):
                row = across(region, hop) * height + goal * rank
                found[(hop - 1) * rank : hop * rank, :] = col[at(row, rank), :]
            outs[step][...] = jnp.dot(found[...], rows, preferred_element_type=f32).astype(bf16)

    parcels = pl.pallas_call(
        pack,
        out_shape=[jax.ShapeDtypeStruct((width, loads), bf16)] * groups,
        in_specs=[HBM] * 3,
        out_specs=[VMEM] * groups,
        scratch_shapes=[
            pltpu.SMEM(cluster_size.shape, cluster_size.dtype),
            pltpu.VMEM((slots, loads), bf16),
            pltpu.VMEM((clusters * rank, slots), bf16),
            pltpu.VMEM((width, slots), bf16),
            pltpu.SemaphoreType.DMA((3,)),
        ],
        compiler_params=PARAMS,
        name="pack",
    )(*(pltpu.with_memory_space_constraint(x, pltpu.HBM) for x in (cluster_size, densities, column_factor)))

    held = [parcels[0]]
    for step in range(1, groups):
        pairs = [(z, (z + step) % groups) for z in range(groups)]
        held.append(lax.ppermute(parcels[step], "sub", pairs))
    ring = folded(groups)
    nearby = [densities]
    for step in range(1, groups):
        pairs = [(ring[p], ring[(p + step) % groups]) for p in range(groups)]
        nearby.append(lax.ppermute(densities, "sub", pairs))

    def fetch(size_hbm, block_hbm, factor_hbm, group_ref, own_ref, block_ref, factor_ref, size, sems):
        copies = [
            pltpu.make_async_copy(source, target, sems.at[i])
            for i, (source, target) in enumerate(
                ((size_hbm, size), (block_hbm, block_ref), (factor_hbm, factor_ref))
            )
        ]
        for copy in copies:
            copy.start()
        sub = lax.axis_index("sub")
        region = lax.axis_index("region")
        slot = lax.broadcasted_iota(jnp.int32, (slots, loads), 0)
        copies[0].wait()
        for g in range(groups):
            keep = slot < size[region * groups + g]
            group_ref[g * slots : (g + 1) * slots, :] = jnp.where(keep, 1.0, 0.0).astype(bf16)
        own_ref[...] = jnp.where(slot < size[region * groups + sub], 1.0, 0.0)
        for copy in copies[1:]:
            copy.wait()

    group_mask, own_mask, near_block, row_factor = pl.pallas_call(
        fetch,
        out_shape=[
            jax.ShapeDtypeStruct((groups * slots, loads), bf16),
            jax.ShapeDtypeStruct((slots, loads), f32),
            jax.ShapeDtypeStruct(near_block.shape, bf16),
            jax.ShapeDtypeStruct(row_factor.shape, bf16),
        ],
        in_specs=[HBM] * 3,
        out_specs=[VMEM] * 4,
        scratch_shapes=[
            pltpu.SMEM(cluster_size.shape, cluster_size.dtype),
            pltpu.SemaphoreType.DMA((3,)),
        ],
        compiler_params=PARAMS,
        cost_estimate=cost(1 << 20),
        name="fetch",
    )(*(pltpu.with_memory_space_constraint(x, pltpu.HBM) for x in (cluster_size, near_block, row_factor)))

    def regroup(*refs):
        ins, outs = refs[:groups], refs[groups:]
        sub = lax.axis_index("sub")
        for step in range(groups):
            for hop in range(1, regions):
                outs[hop - 1][at(behind(sub, step) * rank, rank), :] = ins[step][(hop - 1) * rank : hop * rank, :]

    letters = pl.pallas_call(
        regroup,
        out_shape=[jax.ShapeDtypeStruct((height, loads), bf16)] * (regions - 1),
        in_specs=[VMEM] * groups,
        out_specs=[VMEM] * (regions - 1),
        compiler_params=PARAMS,
        cost_estimate=cost(1 << 16),
        name="regroup",
    )(*held)

    received = {}
    for hop in hops:
        pairs = [(r, r ^ hop) for r in range(regions)]
        received[hop] = lax.ppermute(letters[hop - 1], "region", pairs)

    late = min(2, regions - 1)
    early = [hop for hop in range(1, regions) if hop != late]

    def far_part(factor_ref, letter, hop):
        start = across(lax.axis_index("region"), hop) * height
        return jnp.dot(factor_ref[:, at(start, height)], letter[...], preferred_element_type=f32)

    def near(block_ref, mask_ref, *refs):
        parcels, out, stack = refs[:groups], refs[groups], refs[groups + 1]
        sub = lax.axis_index("sub")
        for step in range(groups):
            origin = sub
            if step:
                for p in range(groups):
                    origin = jnp.where(sub == ring[p], ring[p - step], origin)
            here = at(origin * slots, slots)
            stack[here, :] = parcels[step][...] * mask_ref[here, :]
        out[...] = jnp.dot(block_ref[...], stack[...], preferred_element_type=f32)

    near_sum = pl.pallas_call(
        near,
        out_shape=jax.ShapeDtypeStruct((slots, loads), f32),
        in_specs=[VMEM] * (groups + 2),
        out_specs=VMEM,
        scratch_shapes=[pltpu.VMEM((groups * slots, loads), bf16)],
        compiler_params=PARAMS,
        cost_estimate=cost(1 << 24),
        name="near",
    )(near_block, group_mask, *nearby)

    def gain(near_ref, factor_ref, *refs):
        total = near_ref[...]
        for hop, letter in zip(early, refs):
            total += far_part(factor_ref, letter, hop)
        refs[-1][...] = total

    partial = pl.pallas_call(
        gain,
        out_shape=jax.ShapeDtypeStruct((slots, loads), f32),
        in_specs=[VMEM] * (len(early) + 2),
        out_specs=VMEM,
        compiler_params=PARAMS,
        cost_estimate=cost(1 << 24),
        name="gain",
    )(near_sum, row_factor, *(received[hop] for hop in early))

    def finish(mask_ref, partial_ref, factor_ref, letter, out):
        total = partial_ref[...] + far_part(factor_ref, letter, late)
        out[...] = jnp.where(mask_ref[...] > 0.0, total, 0.0)

    return pl.pallas_call(
        finish,
        out_shape=jax.ShapeDtypeStruct((slots, loads), f32),
        in_specs=[VMEM] * 4,
        out_specs=VMEM,
        compiler_params=PARAMS,
        cost_estimate=cost(1 << 24),
        name="finish",
    )(own_mask, partial, row_factor, received[late])


def solution(mesh):
    spec = P(("sample", "region", "sub"), None)
    return jax.shard_map(
        local,
        mesh=mesh,
        in_specs=(spec, P("sample"), spec, spec, P(None, ("sample", "region", "sub"))),
        out_specs=spec,
        check_vma=False,
    )
```

time: 17.7 us -> 18.1 us (1.023)
  starting transfers between devices: 9.19 us -> 12.3 us
  waiting for transfers between devices: 5.33 us -> 2.34 us
  Pallas kernels: 2.88 us -> 3.27 us
    ppermute x0 -> x3, starting transfers between devices: none -> 5 us  [local(): nearby.append(lax.ppermute(densities, 'sub', pairs))]
    ppermute x3, starting transfers between devices: 7.04 us -> 5.08 us  [local(): held.append(lax.ppermute(parcels[step], 'sub', pairs))]
    ppermute x3, waiting for transfers between devices: 2.26 us -> 0.35 us  [local(): held.append(lax.ppermute(parcels[step], 'sub', pairs))]
    ppermute x3, waiting for transfers between devices: 3.07 us -> 1.46 us  [local(): received[hop] = lax.ppermute(letters[hop - 1], 'region', pairs)]
    ppermute x0 -> x3, waiting for transfers between devices: none -> 0.53 us  [local(): nearby.append(lax.ppermute(densities, 'sub', pairs))]
    pallas_call x4 -> x3, Pallas kernels: 1.74 us -> 2.13 us  [the longest x1 1.12 us: local(): pl.pallas_call(pack, out_shape=[jax.ShapeDtypeStruct((width, loads), bf16...]
  transfers between devices with their start and end apart: 6 -> 9, of which waited for: 4 -> 4; matrix products, arithmetic and copies ran while one was open for 0% -> 0% of each run, Pallas kernels for 6% -> 14%
where the time goes in v4:
time: 18.1 us; the launch traced here: 18 us
  starting transfers between devices  12.3 us (68%)
  Pallas kernels  3.27 us (18%)
  waiting for transfers between devices  2.34 us (13%)
    ppermute x3, starting transfers between devices, local(): held.append(lax.ppermute(parcels[step], 'sub', pairs))  5.08 us
    ppermute x3, starting transfers between devices, local(): nearby.append(lax.ppermute(densities, 'sub', pairs))  5 us
    ppermute x3, starting transfers between devices, local(): received[hop] = lax.ppermute(letters[hop - 1], 'region', pairs)  2.2 us
    ppermute x3, waiting for transfers between devices, local(): received[hop] = lax.ppermute(letters[hop - 1], 'region', pairs)  1.46 us
    pallas_call x1, Pallas kernels, local(): pl.pallas_call(pack, out_shape=[jax.ShapeDtypeStruct((width, loads), bf16...  1.12 us
    pallas_call x1, Pallas kernels, local(): pl.pallas_call(fetch, out_shape=[jax.ShapeDtypeStruct((groups * slots, lo...  0.99 us
    pallas_call x1, Pallas kernels, local(): pl.pallas_call(finish, out_shape=jax.ShapeDtypeStruct((slots, loads), f32...  0.77 us
    ppermute x3, waiting for transfers between devices, local(): nearby.append(lax.ppermute(densities, 'sub', pairs))  0.53 us
  transfers between devices with their start and end apart: 9, of which 4 were waited for; matrix products, arithmetic and copies ran while one was open for 0% of the time, Pallas kernels for 14%

profile of v4, /device:TPU:0, one launch (start us, length us, event | category | flops | bytes accessed | tf_op | source)
XLA Modules:
  0.0 18.0 jit_solution(10396383121458888988)
XLA Ops:
  0.0 0.0 copy-start
  0.0 3.1 %collective-permute-start = (bf16[128,128]{1,0:T(8,128)(2,1)}, bf16[128,128]{1,0:T(8,128)(2,1)S(1)}, u32[]{:S(2)}, u32[]{:S(2)}) collective-permute-start(bf16[128,128]{1,0:T(8,128)(2,1)} %dens_hbm.1), channel_id=1, source_target_pairs={{0,1},{1,3},{3,2},{2,0},{4,5},{5,7},{7,6},{6,4},{8,9},{9,11},{11,1... | collective-permute-start | bytes 98312 | tf_op jit(solution)/shard_map/ppermute | solution.py:95
  3.1 1.1 %pack.1 = (bf16[96,128]{1,0:T(8,128)(2,1)S(1)}, bf16[96,128]{1,0:T(8,128)(2,1)S(1)}, bf16[96,128]{1,0:T(8,128)(2,1)S(1)}, bf16[96,128]{1,0:T(8,128)(2,1)S(1)}) custom-call(s32[16]{0:T(128)} %size_hbm.3, bf16[128,128]{1,0:T(8,128)(2,1)} %dens_hbm.1, bf16[512,128]{1,0:T(8,128)(2,1)} %col_hbm.1), custom_call_target="tpu_custom_call" | custom-call | tf_op jit(solution)/shard_map/pack/pallas_call | solution.py:71
  4.2 2.6 %collective-permute-start.3 = (bf16[96,128]{1,0:T(8,128)(2,1)S(1)}, bf16[96,128]{1,0:T(8,128)(2,1)S(1)}, u32[]{:S(2)}, u32[]{:S(2)}) collective-permute-start(bf16[96,128]{1,0:T(8,128)(2,1)S(1)} %get-tuple-element.21), channel_id=1, source_target_pairs={{0,1},{1,2},{2,3},{3,0},{4,5},{5,6},{6,7},{7,4},{8,9},{9,10},{10,1... | collective-permute-start | bytes 73736 | tf_op jit(solution)/shard_map/ppermute | solution.py:90
  6.8 0.4 %collective-permute-start.4 = (bf16[96,128]{1,0:T(8,128)(2,1)S(1)}, bf16[96,128]{1,0:T(8,128)(2,1)S(1)}, u32[]{:S(2)}, u32[]{:S(2)}) collective-permute-start(bf16[96,128]{1,0:T(8,128)(2,1)S(1)} %get-tuple-element.22), channel_id=1, source_target_pairs={{0,2},{1,3},{2,0},{3,1},{4,6},{5,7},{6,4},{7,5},{8,10},{9,11},{10,... | collective-permute-start | bytes 73736 | tf_op jit(solution)/shard_map/ppermute | solution.py:90
  7.3 2.0 %collective-permute-start.5 = (bf16[96,128]{1,0:T(8,128)(2,1)S(1)}, bf16[96,128]{1,0:T(8,128)(2,1)S(1)}, u32[]{:S(2)}, u32[]{:S(2)}) collective-permute-start(bf16[96,128]{1,0:T(8,128)(2,1)S(1)} %get-tuple-element.23), channel_id=1, source_target_pairs={{0,3},{1,0},{2,1},{3,2},{4,7},{5,4},{6,5},{7,6},{8,11},{9,8},{10,9... | collective-permute-start | bytes 73736 | tf_op jit(solution)/shard_map/ppermute | solution.py:90
  9.3 0.0 copy-done
  9.3 1.9 %collective-permute-start.1 = (bf16[128,128]{1,0:T(8,128)(2,1)S(1)}, bf16[128,128]{1,0:T(8,128)(2,1)S(1)}, u32[]{:S(2)}, u32[]{:S(2)}) collective-permute-start(bf16[128,128]{1,0:T(8,128)(2,1)S(1)} %copy-done), channel_id=1, source_target_pairs={{0,3},{1,2},{3,0},{2,1},{4,7},{5,6},{7,4},{6,5},{8,11},{9,10},{11,... | collective-permute-start | bytes 98312 | tf_op jit(solution)/shard_map/ppermute | solution.py:95
  11.2 0.0 collective-permute-done.3.refs_1_
  11.2 0.0 collective-permute-start.2
  11.2 0.3 %collective-permute-done.4.refs_2_ = bf16[96,128]{1,0:T(8,128)(2,1)S(1)} collective-permute-done((bf16[96,128]{1,0:T(8,128)(2,1)S(1)}, bf16[96,128]{1,0:T(8,128)(2,1)S(1)}, u32[]{:S(2)}, u32[]{:S(2)}) %collective-permute-start.4) | collective-permute-done | bytes 24608 | tf_op jit(solution)/shard_map/ppermute | solution.py:90
  11.6 0.0 collective-permute-done.5.refs_3_
  11.6 0.1 collective-permute-start.6
  11.7 1.6 %collective-permute-start.7 = (bf16[128,128]{1,0:T(8,128)(2,1)S(1)}, bf16[128,128]{1,0:T(8,128)(2,1)S(1)}, u32[]{:S(2)}, u32[]{:S(2)}) collective-permute-start(bf16[128,128]{1,0:T(8,128)(2,1)S(1)} %get-tuple-element.25), channel_id=1, source_target_pairs={{0,12},{4,8},{8,4},{12,0},{1,13},{5,9},{9,5},{13,1},{2,14},{6,10},... | collective-permute-start | bytes 98312 | tf_op jit(solution)/shard_map/ppermute | solution.py:156
  13.3 0.0 collective-permute-done.refs_1_
  13.3 0.5 %collective-permute-start.8 = (bf16[128,128]{1,0:T(8,128)(2,1)S(1)}, bf16[128,128]{1,0:T(8,128)(2,1)S(1)}, u32[]{:S(2)}, u32[]{:S(2)}) collective-permute-start(bf16[128,128]{1,0:T(8,128)(2,1)S(1)} %get-tuple-element.26), channel_id=1, source_target_pairs={{0,8},{4,12},{8,0},{12,4},{1,9},{5,13},{9,1},{13,5},{2,10},{6,14},... | collective-permute-start | bytes 98312 | tf_op jit(solution)/shard_map/ppermute | solution.py:156
  13.8 1.0 %fetch.1 = (bf16[512,128]{1,0:T(8,128)(2,1)S(1)}, f32[128,128]{1,0:T(8,128)S(1)}, bf16[128,512]{1,0:T(8,128)(2,1)S(1)}, bf16[128,512]{1,0:T(8,128)(2,1)S(1)}) custom-call(s32[16]{0:T(128)} %size_hbm.3, bf16[128,512]{1,0:T(8,128)(2,1)} %block_hbm.1, bf16[128,512]{1,0:T(8,128)(2,1)} %factor_hbm.1), custom_call_target="tpu_custom_call" | custom-call | flops 1048576 | tf_op jit(solution)/shard_map/fetch/pallas_call | solution.py:117
  14.8 0.2 %collective-permute-done.1.refs_2_ = bf16[128,128]{1,0:T(8,128)(2,1)S(1)} collective-permute-done((bf16[128,128]{1,0:T(8,128)(2,1)S(1)}, bf16[128,128]{1,0:T(8,128)(2,1)S(1)}, u32[]{:S(2)}, u32[]{:S(2)}) %collective-permute-start.1) | collective-permute-done | bytes 32800 | tf_op jit(solution)/shard_map/ppermute | solution.py:95
  15.0 0.3 %collective-permute-done.2.refs_3_ = bf16[128,128]{1,0:T(8,128)(2,1)S(1)} collective-permute-done((bf16[128,128]{1,0:T(8,128)(2,1)S(1)}, bf16[128,128]{1,0:T(8,128)(2,1)S(1)}, u32[]{:S(2)}, u32[]{:S(2)}) %collective-permute-start.2) | collective-permute-done | bytes 32800 | tf_op jit(solution)/shard_map/ppermute | solution.py:95
  15.3 0.2 %near.1.near_ref = f32[128,128]{1,0:T(8,128)S(1)} custom-call(bf16[128,512]{1,0:T(8,128)(2,1)S(1)} %get-tuple-element.17.block_ref, bf16[512,128]{1,0:T(8,128)(2,1)S(1)} %get-tuple-element.18.mask_ref, bf16[128,128]{1,0:T(8,128)(2,1)S(1)} %copy-done, bf16[128,128]{1,0:T(8,128)(2,1)S(1)} %collective-permute-done.refs_1_, ...), custom_call_target="tpu_custom_call" | custom-call | flops 16777216 | tf_op jit(solution)/shard_map/near/pallas_call | solution.py:177
  15.6 0.0 collective-permute-done.6.refs_0_
  15.6 0.0 collective-permute-done.7.refs_1_
  15.6 0.2 gain.1.partial_ref
  15.7 1.5 %collective-permute-done.8.letter = bf16[128,128]{1,0:T(8,128)(2,1)S(1)} collective-permute-done((bf16[128,128]{1,0:T(8,128)(2,1)S(1)}, bf16[128,128]{1,0:T(8,128)(2,1)S(1)}, u32[]{:S(2)}, u32[]{:S(2)}) %collective-permute-start.8) | collective-permute-done | bytes 32800 | tf_op jit(solution)/shard_map/ppermute | solution.py:156
  17.2 0.8 %finish.1 = f32[128,128]{1,0:T(8,128)} custom-call(f32[128,128]{1,0:T(8,128)S(1)} %get-tuple-element.16.mask_ref, f32[128,128]{1,0:T(8,128)S(1)} %gain.1.partial_ref, bf16[128,512]{1,0:T(8,128)(2,1)S(1)} %get-tuple-element.19.factor_ref, bf16[128,128]{1,0:T(8,128)(2,1)S(1)} %collective-permute-done.8.letter), custom_call_target="tpu_custom_call" | custom-call | flops 16777216 | tf_op jit(solution)/shard_map/finish/pallas_call | solution.py:208
  (1 shorter events, 0.0 us)
Async XLA Ops:
  0.0 9.3 %copy-start = (bf16[128,128]{1,0:T(8,128)(2,1)S(1)}, bf16[128,128]{1,0:T(8,128)(2,1)}, u32[]{:S(2)}) copy-start(bf16[128,128]{1,0:T(8,128)(2,1)} %dens_hbm.1) | copy-start | bytes 98308
  0.0 13.3 %collective-permute-start = (bf16[128,128]{1,0:T(8,128)(2,1)}, bf16[128,128]{1,0:T(8,128)(2,1)S(1)}, u32[]{:S(2)}, u32[]{:S(2)}) collective-permute-start(bf16[128,128]{1,0:T(8,128)(2,1)} %dens_hbm.1), channel_id=1, source_target_pairs={{0,1},{1,3},{3,2},{2,0},{4,5},{5,7},{7,6},{6,4},{8,9},{9,11},{11,1... | collective-permute-start | bytes 98312 | tf_op jit(solution)/shard_map/ppermute | solution.py:95
  4.2 7.0 %collective-permute-start.3 = (bf16[96,128]{1,0:T(8,128)(2,1)S(1)}, bf16[96,128]{1,0:T(8,128)(2,1)S(1)}, u32[]{:S(2)}, u32[]{:S(2)}) collective-permute-start(bf16[96,128]{1,0:T(8,128)(2,1)S(1)} %get-tuple-element.21), channel_id=1, source_target_pairs={{0,1},{1,2},{2,3},{3,0},{4,5},{5,6},{6,7},{7,4},{8,9},{9,10},{10,1... | collective-permute-start | bytes 73736 | tf_op jit(solution)/shard_map/ppermute | solution.py:90
  6.8 4.7 %collective-permute-start.4 = (bf16[96,128]{1,0:T(8,128)(2,1)S(1)}, bf16[96,128]{1,0:T(8,128)(2,1)S(1)}, u32[]{:S(2)}, u32[]{:S(2)}) collective-permute-start(bf16[96,128]{1,0:T(8,128)(2,1)S(1)} %get-tuple-element.22), channel_id=1, source_target_pairs={{0,2},{1,3},{2,0},{3,1},{4,6},{5,7},{6,4},{7,5},{8,10},{9,11},{10,... | collective-permute-start | bytes 73736 | tf_op jit(solution)/shard_map/ppermute | solution.py:90
  7.3 4.3 %collective-permute-start.5 = (bf16[96,128]{1,0:T(8,128)(2,1)S(1)}, bf16[96,128]{1,0:T(8,128)(2,1)S(1)}, u32[]{:S(2)}, u32[]{:S(2)}) collective-permute-start(bf16[96,128]{1,0:T(8,128)(2,1)S(1)} %get-tuple-element.23), channel_id=1, source_target_pairs={{0,3},{1,0},{2,1},{3,2},{4,7},{5,4},{6,5},{7,6},{8,11},{9,8},{10,9... | collective-permute-start | bytes 73736 | tf_op jit(solution)/shard_map/ppermute | solution.py:90
  9.3 5.7 %collective-permute-start.1 = (bf16[128,128]{1,0:T(8,128)(2,1)S(1)}, bf16[128,128]{1,0:T(8,128)(2,1)S(1)}, u32[]{:S(2)}, u32[]{:S(2)}) collective-permute-start(bf16[128,128]{1,0:T(8,128)(2,1)S(1)} %copy-done), channel_id=1, source_target_pairs={{0,3},{1,2},{3,0},{2,1},{4,7},{5,6},{7,4},{6,5},{8,11},{9,10},{11,... | collective-permute-start | bytes 98312 | tf_op jit(solution)/shard_map/ppermute | solution.py:95
  11.2 4.1 %collective-permute-start.2 = (bf16[128,128]{1,0:T(8,128)(2,1)S(1)}, bf16[128,128]{1,0:T(8,128)(2,1)S(1)}, u32[]{:S(2)}, u32[]{:S(2)}) collective-permute-start(bf16[128,128]{1,0:T(8,128)(2,1)S(1)} %copy-done), channel_id=1, source_target_pairs={{0,2},{1,0},{3,1},{2,3},{4,6},{5,4},{7,5},{6,7},{8,10},{9,8},{11,9... | collective-permute-start | bytes 98312 | tf_op jit(solution)/shard_map/ppermute | solution.py:95
  11.6 4.0 %collective-permute-start.6 = (bf16[128,128]{1,0:T(8,128)(2,1)S(1)}, bf16[128,128]{1,0:T(8,128)(2,1)S(1)}, u32[]{:S(2)}, u32[]{:S(2)}) collective-permute-start(bf16[128,128]{1,0:T(8,128)(2,1)S(1)} %get-tuple-element.24), channel_id=1, source_target_pairs={{0,4},{4,0},{8,12},{12,8},{1,5},{5,1},{9,13},{13,9},{2,6},{6,2},{1... | collective-permute-start | bytes 98312 | tf_op jit(solution)/shard_map/ppermute | solution.py:156
  11.7 3.9 %collective-permute-start.7 = (bf16[128,128]{1,0:T(8,128)(2,1)S(1)}, bf16[128,128]{1,0:T(8,128)(2,1)S(1)}, u32[]{:S(2)}, u32[]{:S(2)}) collective-permute-start(bf16[128,128]{1,0:T(8,128)(2,1)S(1)} %get-tuple-element.25), channel_id=1, source_target_pairs={{0,12},{4,8},{8,4},{12,0},{1,13},{5,9},{9,5},{13,1},{2,14},{6,10},... | collective-permute-start | bytes 98312 | tf_op jit(solution)/shard_map/ppermute | solution.py:156
  13.3 3.9 %collective-permute-start.8 = (bf16[128,128]{1,0:T(8,128)(2,1)S(1)}, bf16[128,128]{1,0:T(8,128)(2,1)S(1)}, u32[]{:S(2)}, u32[]{:S(2)}) collective-permute-start(bf16[128,128]{1,0:T(8,128)(2,1)S(1)} %get-tuple-element.26), channel_id=1, source_target_pairs={{0,8},{4,12},{8,0},{12,4},{1,9},{5,13},{9,1},{13,5},{2,10},{6,14},... | collective-permute-start | bytes 98312 | tf_op jit(solution)/shard_map/ppermute | solution.py:156

commit v5 on v3

--- a/solution.py
+++ b/solution.py
@@ -41,34 +41,34 @@
         return lax.bitwise_xor(region, jnp.int32(hop))
 
     def gather(dens, col, *refs):
-        outs, (dens_buf, col_buf, sems) = refs[:groups], refs[groups:]
+        outs, (dens_buf, col_buf, sems) = refs[: groups - 1], refs[groups - 1 :]
         sub = lax.axis_index("sub")
         region = lax.axis_index("region")
         first = pltpu.make_async_copy(dens, dens_buf, sems.at[0])
+        copies = []
+        for step in range(1, groups):
+            goal = ahead(sub, step)
+            copies.append(pltpu.make_async_copy(col.at[:, goal], col_buf.at[step - 1], sems.at[1]))
+            copies[-1].start()
         first.start()
-        copies = []
-        for step in range(groups):
-            goal = ahead(sub, step)
-            copies.append(pltpu.make_async_copy(col.at[:, goal], col_buf.at[step], sems.at[1]))
-            copies[-1].start()
         first.wait()
-        for step in range(groups):
-            outs[step][0:slots, :] = dens_buf[...]
+        for out in outs:
+            out[0:slots, :] = dens_buf[...]
         for copy in copies:
             copy.wait()
-        for step in range(groups):
+        for i, out in enumerate(outs):
             for hop in range(1, regions):
                 low = slots + (hop - 1) * rank
-                outs[step][low : low + rank, :] = col_buf[step, across(region, hop)]
+                out[low : low + rank, :] = col_buf[i, across(region, hop)]
 
     parcels = pl.pallas_call(
         gather,
-        out_shape=[jax.ShapeDtypeStruct((slots + width, loads), bf16)] * groups,
+        out_shape=[jax.ShapeDtypeStruct((slots + width, loads), bf16)] * (groups - 1),
         in_specs=[HBM] * 2,
-        out_specs=[VMEM] * groups,
+        out_specs=[VMEM] * (groups - 1),
         scratch_shapes=[
             pltpu.VMEM((slots, loads), bf16),
-            pltpu.VMEM((groups, regions, rank, slots), bf16),
+            pltpu.VMEM((groups - 1, regions, rank, slots), bf16),
             pltpu.SemaphoreType.DMA((2,)),
         ],
         compiler_params=PARAMS,
@@ -78,10 +78,10 @@
         pltpu.with_memory_space_constraint(column_factor.reshape(regions, groups, rank, slots), pltpu.HBM),
     )
 
-    held = [parcels[0]]
+    held = []
     for step in range(1, groups):
         pairs = [(z, (z + step) % groups) for z in range(groups)]
-        held.append(lax.ppermute(parcels[step], "sub", pairs))
+        held.append(lax.ppermute(parcels[step - 1], "sub", pairs))
 
     def mask(size_ref, group_ref, own_ref):
         sub = lax.axis_index("sub")
@@ -113,9 +113,16 @@
         for hop in range(1, regions):
             outs[hop - 1][at(origin * rank, rank), :] = part[(hop - 1) * rank : hop * rank, :]
 
-    def regroup(mask_ref, *refs):
-        for step in range(groups - 1):
-            weigh(step, mask_ref, refs[step], refs[groups - 1 :])
+    def regroup(mask_ref, dens_ref, col_ref, *refs):
+        parcels, outs, own = refs[: groups - 2], refs[groups - 2 : -1], refs[-1]
+        sub = lax.axis_index("sub")
+        region = lax.axis_index("region")
+        own[0:slots, :] = dens_ref[...]
+        for hop in range(1, regions):
+            low = slots + (hop - 1) * rank
+            own[low : low + rank, :] = col_ref[across(region, hop), sub]
+        for step, parcel in enumerate((own, *parcels)):
+            weigh(step, mask_ref, parcel, outs)
 
     def complete(mask_ref, parcel, *refs):
         begun, outs = refs[: regions - 1], refs[regions - 1 :]
@@ -127,12 +134,13 @@
     letters = pl.pallas_call(
         regroup,
         out_shape=letter_shapes,
-        in_specs=[VMEM] * groups,
+        in_specs=[VMEM] * (groups + 1),
         out_specs=[VMEM] * (regions - 1),
+        scratch_shapes=[pltpu.VMEM((slots + width, loads), bf16)],
         compiler_params=PARAMS,
         cost_estimate=cost(1 << 20),
         name="regroup",
-    )(group_mask, *held[:-1])
+    )(group_mask, densities, column_factor.reshape(regions, groups, rank, slots), *held[:-1])
     letters = pl.pallas_call(
         complete,
         out_shape=letter_shapes,
@@ -172,7 +180,7 @@
         compiler_params=PARAMS,
         cost_estimate=cost(1 << 24),
         name="near",
-    )(near_block, group_mask, *held)
+    )(near_block, group_mask, densities, *held)
 
     def gain(near_ref, factor_ref, *refs):
         total = near_ref[...]

time: 17.7 us -> 17.7 us (level)
  no operation moved by 1% of the time
where the time goes in v5:
time: 17.7 us; the launch traced here: 17.5 us
  starting transfers between devices  9.19 us (52%)
  waiting for transfers between devices  5.33 us (30%)
  Pallas kernels  2.92 us (16%)
    ppermute x3, starting transfers between devices, local(): held.append(lax.ppermute(parcels[step - 1], 'sub', pairs))  7.04 us
    ppermute x3, waiting for transfers between devices, local(): received[hop] = lax.ppermute(letters[hop - 1], 'region', pairs)  3.08 us
    ppermute x3, waiting for transfers between devices, local(): held.append(lax.ppermute(parcels[step - 1], 'sub', pairs))  2.25 us
    ppermute x3, starting transfers between devices, local(): received[hop] = lax.ppermute(letters[hop - 1], 'region', pairs)  2.14 us
    pallas_call x1, Pallas kernels, local(): pl.pallas_call(gather, out_shape=[jax.ShapeDtypeStruct((slots + width, lo...  0.88 us
    pallas_call x1, Pallas kernels, local(): pl.pallas_call(finish, out_shape=jax.ShapeDtypeStruct((slots, loads), f32...  0.77 us
    pallas_call x1, Pallas kernels, local(): pl.pallas_call(mask, out_shape=[jax.ShapeDtypeStruct((groups * slots, loa...  0.59 us
  transfers between devices with their start and end apart: 6, of which 4 were waited for; matrix products, arithmetic and copies ran while one was open for 0% of the time, Pallas kernels for 6%

profile of v5, /device:TPU:0, one launch (start us, length us, event | category | flops | bytes accessed | tf_op | source)
XLA Modules:
  0.0 17.5 jit_solution(3187730247456828682)
XLA Ops:
  0.0 0.0 copy-start
  0.0 0.0 copy-start.2
  0.0 0.9 %gather.1 = (bf16[224,128]{1,0:T(8,128)(2,1)S(1)}, bf16[224,128]{1,0:T(8,128)(2,1)S(1)}, bf16[224,128]{1,0:T(8,128)(2,1)S(1)}) custom-call(bf16[128,128]{1,0:T(8,128)(2,1)} %dens_ref.1, bf16[4,4,32,128]{3,2,1,0:T(8,128)(2,1)} %bitcast.1), custom_call_target="tpu_custom_call" | custom-call | tf_op jit(solution)/shard_map/gather/pallas_call | solution.py:64
  0.9 3.1 %collective-permute-start = (bf16[224,128]{1,0:T(8,128)(2,1)S(1)}, bf16[224,128]{1,0:T(8,128)(2,1)S(1)}, u32[]{:S(2)}, u32[]{:S(2)}) collective-permute-start(bf16[224,128]{1,0:T(8,128)(2,1)S(1)} %get-tuple-element.18), channel_id=1, source_target_pairs={{0,1},{1,2},{2,3},{3,0},{4,5},{5,6},{6,7},{7,4},{8,9},{9,10},{10,1... | collective-permute-start | bytes 172040 | tf_op jit(solution)/shard_map/ppermute | solution.py:84
  4.0 0.0 copy-start.4
  4.0 2.6 %collective-permute-start.1 = (bf16[224,128]{1,0:T(8,128)(2,1)S(1)}, bf16[224,128]{1,0:T(8,128)(2,1)S(1)}, u32[]{:S(2)}, u32[]{:S(2)}) collective-permute-start(bf16[224,128]{1,0:T(8,128)(2,1)S(1)} %get-tuple-element.19), channel_id=1, source_target_pairs={{0,2},{1,3},{2,0},{3,1},{4,6},{5,7},{6,4},{7,5},{8,10},{9,11},{10,... | collective-permute-start | bytes 172040 | tf_op jit(solution)/shard_map/ppermute | solution.py:84
  6.6 1.3 %collective-permute-start.2 = (bf16[224,128]{1,0:T(8,128)(2,1)S(1)}, bf16[224,128]{1,0:T(8,128)(2,1)S(1)}, u32[]{:S(2)}, u32[]{:S(2)}) collective-permute-start(bf16[224,128]{1,0:T(8,128)(2,1)S(1)} %get-tuple-element.20), channel_id=1, source_target_pairs={{0,3},{1,0},{2,1},{3,2},{4,7},{5,4},{6,5},{7,6},{8,11},{9,8},{10,9... | collective-permute-start | bytes 172040 | tf_op jit(solution)/shard_map/ppermute | solution.py:84
  7.9 0.0 copy-done.4
  7.9 0.6 %mask.1 = (bf16[512,128]{1,0:T(8,128)(2,1)S(1)}, f32[128,128]{1,0:T(8,128)S(1)}) custom-call(s32[16]{0:T(128)S(1)} %copy-done.4), custom_call_target="tpu_custom_call" | custom-call | flops 1048576 | tf_op jit(solution)/shard_map/mask/pallas_call | solution.py:95
  8.5 0.0 collective-permute-done.refs_1_.refs_0_
  8.5 2.1 %collective-permute-done.1.refs_2_.refs_1_ = bf16[224,128]{1,0:T(8,128)(2,1)S(1)} collective-permute-done((bf16[224,128]{1,0:T(8,128)(2,1)S(1)}, bf16[224,128]{1,0:T(8,128)(2,1)S(1)}, u32[]{:S(2)}, u32[]{:S(2)}) %collective-permute-start.1) | collective-permute-done | bytes 57376 | tf_op jit(solution)/shard_map/ppermute | solution.py:84
  10.6 0.0 copy-done
  10.6 0.0 copy-done.2
  10.6 0.2 %regroup.1 = (bf16[128,128]{1,0:T(8,128)(2,1)S(1)}, bf16[128,128]{1,0:T(8,128)(2,1)S(1)}, bf16[128,128]{1,0:T(8,128)(2,1)S(1)}) custom-call(bf16[512,128]{1,0:T(8,128)(2,1)S(1)} %get-tuple-element.17.mask_ref, bf16[128,128]{1,0:T(8,128)(2,1)S(1)} %copy-done.2, bf16[4,4,32,128]{3,2,1,0:T(8,128)(2,1)S(1)} %bitcast.2, ...), custom_call_target="tpu_custom_call" | custom-call | flops 1048576 | tf_op jit(solution)/shard_map/regroup/pallas_call | solution.py:134
  10.8 0.2 collective-permute-done.2.refs_3_.parcel
  11.0 0.0 copy-start.3
  11.0 0.1 complete.1
  11.1 0.0 collective-permute-start.3
  11.1 1.7 %collective-permute-start.4 = (bf16[128,128]{1,0:T(8,128)(2,1)S(1)}, bf16[128,128]{1,0:T(8,128)(2,1)S(1)}, u32[]{:S(2)}, u32[]{:S(2)}) collective-permute-start(bf16[128,128]{1,0:T(8,128)(2,1)S(1)} %get-tuple-element.25), channel_id=1, source_target_pairs={{0,12},{4,8},{8,4},{12,0},{1,13},{5,9},{9,5},{13,1},{2,14},{6,10},... | collective-permute-start | bytes 98312 | tf_op jit(solution)/shard_map/ppermute | solution.py:157
  12.8 0.0 copy-start.1
  12.8 0.4 %collective-permute-start.5 = (bf16[128,128]{1,0:T(8,128)(2,1)S(1)}, bf16[128,128]{1,0:T(8,128)(2,1)S(1)}, u32[]{:S(2)}, u32[]{:S(2)}) collective-permute-start(bf16[128,128]{1,0:T(8,128)(2,1)S(1)} %get-tuple-element.26), channel_id=1, source_target_pairs={{0,8},{4,12},{8,0},{12,4},{1,9},{5,13},{9,1},{13,5},{2,10},{6,14},... | collective-permute-start | bytes 98312 | tf_op jit(solution)/shard_map/ppermute | solution.py:157
  13.3 0.0 copy-done.3
  13.3 0.2 %near.1.near_ref = f32[128,128]{1,0:T(8,128)S(1)} custom-call(bf16[128,512]{1,0:T(8,128)(2,1)S(1)} %copy-done.3, bf16[512,128]{1,0:T(8,128)(2,1)S(1)} %get-tuple-element.17.mask_ref, bf16[128,128]{1,0:T(8,128)(2,1)S(1)} %copy-done.2, bf16[224,128]{1,0:T(8,128)(2,1)S(1)} %collective-permute-done.refs_1_.refs_0_, ...), custom_call_target="tpu_custom_call" | custom-call | flops 16777216 | tf_op jit(solution)/shard_map/near/pallas_call | solution.py:174
  13.5 0.0 collective-permute-done.3.refs_0_
  13.5 1.0 %collective-permute-done.4.refs_1_ = bf16[128,128]{1,0:T(8,128)(2,1)S(1)} collective-permute-done((bf16[128,128]{1,0:T(8,128)(2,1)S(1)}, bf16[128,128]{1,0:T(8,128)(2,1)S(1)}, u32[]{:S(2)}, u32[]{:S(2)}) %collective-permute-start.4) | collective-permute-done | bytes 32800 | tf_op jit(solution)/shard_map/ppermute | solution.py:157
  14.6 0.0 copy-done.1
  14.6 0.2 gain.1.partial_ref
  14.7 2.0 %collective-permute-done.5.letter = bf16[128,128]{1,0:T(8,128)(2,1)S(1)} collective-permute-done((bf16[128,128]{1,0:T(8,128)(2,1)S(1)}, bf16[128,128]{1,0:T(8,128)(2,1)S(1)}, u32[]{:S(2)}, u32[]{:S(2)}) %collective-permute-start.5) | collective-permute-done | bytes 32800 | tf_op jit(solution)/shard_map/ppermute | solution.py:157
  16.8 0.8 %finish.1 = f32[128,128]{1,0:T(8,128)} custom-call(f32[128,128]{1,0:T(8,128)S(1)} %get-tuple-element.16.mask_ref, f32[128,128]{1,0:T(8,128)S(1)} %gain.1.partial_ref, bf16[128,512]{1,0:T(8,128)(2,1)S(1)} %copy-done.1, bf16[128,128]{1,0:T(8,128)(2,1)S(1)} %collective-permute-done.5.letter), custom_call_target="tpu_custom_call" | custom-call | flops 16777216 | tf_op jit(solution)/shard_map/finish/pallas_call | solution.py:205
Async XLA Ops:
  0.0 10.6 %copy-start = (bf16[512,128]{1,0:T(8,128)(2,1)S(1)}, bf16[512,128]{1,0:T(8,128)(2,1)}, u32[]{:S(2)}) copy-start(bf16[512,128]{1,0:T(8,128)(2,1)} %param.9) | copy-start | bytes 393220
  0.0 10.6 %copy-start.2 = (bf16[128,128]{1,0:T(8,128)(2,1)S(1)}, bf16[128,128]{1,0:T(8,128)(2,1)}, u32[]{:S(2)}) copy-start(bf16[128,128]{1,0:T(8,128)(2,1)} %dens_ref.1) | copy-start | bytes 98308
  0.9 7.6 %collective-permute-start = (bf16[224,128]{1,0:T(8,128)(2,1)S(1)}, bf16[224,128]{1,0:T(8,128)(2,1)S(1)}, u32[]{:S(2)}, u32[]{:S(2)}) collective-permute-start(bf16[224,128]{1,0:T(8,128)(2,1)S(1)} %get-tuple-element.18), channel_id=1, source_target_pairs={{0,1},{1,2},{2,3},{3,0},{4,5},{5,6},{6,7},{7,4},{8,9},{9,10},{10,1... | collective-permute-start | bytes 172040 | tf_op jit(solution)/shard_map/ppermute | solution.py:84
  4.0 3.9 %copy-start.4 = (s32[16]{0:T(128)S(1)}, s32[16]{0:T(128)}, u32[]{:S(2)}) copy-start(s32[16]{0:T(128)} %size_ref.1) | copy-start | bytes 196
  4.0 6.6 %collective-permute-start.1 = (bf16[224,128]{1,0:T(8,128)(2,1)S(1)}, bf16[224,128]{1,0:T(8,128)(2,1)S(1)}, u32[]{:S(2)}, u32[]{:S(2)}) collective-permute-start(bf16[224,128]{1,0:T(8,128)(2,1)S(1)} %get-tuple-element.19), channel_id=1, source_target_pairs={{0,2},{1,3},{2,0},{3,1},{4,6},{5,7},{6,4},{7,5},{8,10},{9,11},{10,... | collective-permute-start | bytes 172040 | tf_op jit(solution)/shard_map/ppermute | solution.py:84
  6.6 4.4 %collective-permute-start.2 = (bf16[224,128]{1,0:T(8,128)(2,1)S(1)}, bf16[224,128]{1,0:T(8,128)(2,1)S(1)}, u32[]{:S(2)}, u32[]{:S(2)}) collective-permute-start(bf16[224,128]{1,0:T(8,128)(2,1)S(1)} %get-tuple-element.20), channel_id=1, source_target_pairs={{0,3},{1,0},{2,1},{3,2},{4,7},{5,4},{6,5},{7,6},{8,11},{9,8},{10,9... | collective-permute-start | bytes 172040 | tf_op jit(solution)/shard_map/ppermute | solution.py:84
  11.0 2.3 %copy-start.3 = (bf16[128,512]{1,0:T(8,128)(2,1)S(1)}, bf16[128,512]{1,0:T(8,128)(2,1)}, u32[]{:S(2)}) copy-start(bf16[128,512]{1,0:T(8,128)(2,1)} %block_ref.1) | copy-start | bytes 393220
  11.1 2.4 %collective-permute-start.3 = (bf16[128,128]{1,0:T(8,128)(2,1)S(1)}, bf16[128,128]{1,0:T(8,128)(2,1)S(1)}, u32[]{:S(2)}, u32[]{:S(2)}) collective-permute-start(bf16[128,128]{1,0:T(8,128)(2,1)S(1)} %get-tuple-element.24), channel_id=1, source_target_pairs={{0,4},{4,0},{8,12},{12,8},{1,5},{5,1},{9,13},{13,9},{2,6},{6,2},{1... | collective-permute-start | bytes 98312 | tf_op jit(solution)/shard_map/ppermute | solution.py:157
  11.1 3.4 %collective-permute-start.4 = (bf16[128,128]{1,0:T(8,128)(2,1)S(1)}, bf16[128,128]{1,0:T(8,128)(2,1)S(1)}, u32[]{:S(2)}, u32[]{:S(2)}) collective-permute-start(bf16[128,128]{1,0:T(8,128)(2,1)S(1)} %get-tuple-element.25), channel_id=1, source_target_pairs={{0,12},{4,8},{8,4},{12,0},{1,13},{5,9},{9,5},{13,1},{2,14},{6,10},... | collective-permute-start | bytes 98312 | tf_op jit(solution)/shard_map/ppermute | solution.py:157
  12.8 1.7 %copy-start.1 = (bf16[128,512]{1,0:T(8,128)(2,1)S(1)}, bf16[128,512]{1,0:T(8,128)(2,1)}, u32[]{:S(2)}) copy-start(bf16[128,512]{1,0:T(8,128)(2,1)} %factor_ref.3) | copy-start | bytes 393220
  12.8 3.9 %collective-permute-start.5 = (bf16[128,128]{1,0:T(8,128)(2,1)S(1)}, bf16[128,128]{1,0:T(8,128)(2,1)S(1)}, u32[]{:S(2)}, u32[]{:S(2)}) collective-permute-start(bf16[128,128]{1,0:T(8,128)(2,1)S(1)} %get-tuple-element.26), channel_id=1, source_target_pairs={{0,8},{4,12},{8,0},{12,4},{1,9},{5,13},{9,1},{13,5},{2,10},{6,14},... | collective-permute-start | bytes 98312 | tf_op jit(solution)/shard_map/ppermute | solution.py:157
